TPU v7x, 32 devices: a whole 2x2x4 slice. The times are simulated.
32 devices in a mesh: seq: 8 (over z, x), tp: 4 (over y, core).
Axes of the slice: x: 2, y: 2, z: 4, core: 2. Of those that a mesh axis runs over, the one named last changes fastest.
Arguments:
- inputs: bfloat16 [2, 3584, 1024], P(None, 'seq'), may hold values from -6 to 6
- memory: bfloat16 [2, 3584, 1024], P(None, 'seq'), may hold values from -6 to 6
- compressed: bfloat16 [2, 3584, 1024], P(None, 'seq'), may hold values from -6 to 6
- boundary: int32 [2, 7], replicated, may hold values from 0 to 512
- links: int32 [2, 7], replicated, may hold values 0 or 1
- gains: float32 [2, 1024], replicated, may hold values from 0.5 to 1.5
- shifts: float32 [2, 1024], replicated, may hold values from -3 to 3
- slopes: float32 [8], P('tp'), may hold values from 0.05 to 1.5
- w_query: bfloat16 [1024, 1024], P(None, 'tp'), may hold values from -0.1875 to 0.1875
- w_key: bfloat16 [1024, 1024], P(None, 'tp'), may hold values from -0.1875 to 0.1875
- w_value: bfloat16 [1024, 1024], P(None, 'tp'), may hold values from -0.1875 to 0.1875
- w_out: bfloat16 [1024, 1024], P('tp'), may hold values from -1 to 1
- w_in: bfloat16 [1024, 4096], P(None, 'tp'), may hold values from -0.1875 to 0.1875
- w_down: bfloat16 [4096, 1024], P('tp'), may hold values from -0.09375 to 0.09375
- w_comp: bfloat16 [3, 1024, 1024], P(None, None, 'tp'), may hold values from -0.109375 to 0.109375
- cot_out: bfloat16 [2, 3584, 1024], P(None, 'seq'), may hold values from -6 to 6
- cot_new: bfloat16 [2, 1232, 1024], P(None, 'seq', 'tp'), may hold values from -6 to 6
Outputs:
- out: bfloat16 [2, 3584, 1024], P(None, 'seq')
- d_input: float32 [2, 3584, 1024], P(None, 'seq')
- d_memory: float32 [2, 3584, 1024], P(None, 'seq')
- d_compressed: float32 [2, 3584, 1024], P(None, 'seq')
- new_compressed: float32 [2, 1232, 1024], P(None, 'seq', 'tp')
- g_gains: float32 [2, 1024], P(None, 'seq')
- g_shifts: float32 [2, 1024], P(None, 'seq')
- g_slopes: float32 [8], P('tp')
- g_query: float32 [1024, 1024], P('seq', 'tp')
- g_key: float32 [1024, 1024], P('seq', 'tp')
- g_value: float32 [1024, 1024], P('seq', 'tp')
- g_out: float32 [1024, 1024], P('tp', 'seq')
- g_in: float32 [1024, 4096], P('seq', 'tp')
- g_down: float32 [4096, 1024], P('tp', 'seq')
- g_comp: float32 [3, 1024, 1024], P(None, 'seq', 'tp')
Inputs may be any that keep to these rules, and one draw needn't show every extreme that they name: boundary[m, s] is the place in segment s of micro-batch m where a new document begins; 512 means none begins in it. links[m, s] is 1 where segment s of micro-batch m continues the document of its memories, else 0.
All inputs are finite; a program needn't handle non-finite values.
Results may differ from a plain program's by a relative error of at most 0.013.
The roundings to bfloat16 on the way count: a program that leaves them out, or rounds other values in their place, can miss the bound.
Values may be sent and summed in bfloat16 or wider, within the bound.
A program may use at most 192 MiB of HBM per device.

v0:
```python
import jax
import jax.numpy as jnp
from jax import lax
from jax.sharding import PartitionSpec as P

HEAD = 128
SEG = 512
CSEG = 176
REACH = 19


norm_eps = 1e-05


def shifted(block, axis, distance):
    devices = range(lax.axis_size(axis))
    route = [(i - distance, i) for i in devices if i - distance in devices]
    return lax.ppermute(block, axis, route)


def dot_plain(matrix_a, matrix_b):
    return jnp.dot(matrix_a, matrix_b, preferred_element_type=jnp.float32)


def dot_first_t(matrix_a, matrix_b):
    return lax.dot_general(
        matrix_a, matrix_b, (((0,), (0,)), ((), ())), preferred_element_type=jnp.float32
    )


def dot_second_t(matrix_a, matrix_b):
    return lax.dot_general(
        matrix_a, matrix_b, (((1,), (1,)), ((), ())), preferred_element_type=jnp.float32
    )


def normalize(rows_in, gain_row, shift_row):
    center = rows_in - jnp.mean(rows_in, axis=-1, keepdims=True)
    inverse = lax.rsqrt(jnp.mean(center * center, axis=-1, keepdims=True) + norm_eps)
    scaled = center * inverse
    return (scaled * gain_row + shift_row, scaled, inverse)


def normalize_back(grad_rows, scaled, inverse, gain_row):
    weighted = grad_rows * gain_row
    first_mean = jnp.mean(weighted, axis=-1, keepdims=True)
    second_mean = jnp.mean(weighted * scaled, axis=-1, keepdims=True)
    grad_input = inverse * (weighted - first_mean - scaled * second_mean)
    return (grad_input, jnp.sum(grad_rows * scaled, axis=0), jnp.sum(grad_rows, axis=0))


def per_device(
    inputs,
    memory,
    compressed,
    boundary,
    links,
    gains,
    shifts,
    slopes,
    w_query,
    w_key,
    w_value,
    w_out,
    w_in,
    w_down,
    w_comp,
    cot_out,
    cot_new,
):
    rows = inputs.shape[1]
    slot_count = cot_new.shape[1]
    local_dim = w_comp.shape[2]
    heads_local = w_query.shape[1] // HEAD
    seq_index = lax.axis_index("seq")
    scale = HEAD ** (-0.5)
    row_ids = jnp.arange(rows, dtype=jnp.int32)
    query_pos = seq_index * rows + row_ids
    prev_pos = (seq_index - 1) * rows + row_ids
    next_pos = (seq_index + 1) * rows + row_ids
    beside_all = jnp.concatenate([prev_pos, query_pos, next_pos])
    key_pos = jnp.concatenate([prev_pos, query_pos, beside_all, beside_all])
    key_kind = jnp.concatenate(
        [
            jnp.zeros((2 * rows,), jnp.int32),
            jnp.ones((3 * rows,), jnp.int32),
            jnp.full((3 * rows,), 2, jnp.int32),
        ]
    )
    query_seg = query_pos // SEG
    query_at = query_pos - query_seg * SEG
    key_seg = key_pos // SEG
    key_at = key_pos - key_seg * SEG
    distance = query_at[:, None] - key_at[None, :] + key_kind[None, :] * SEG
    reach_term = -distance.astype(jnp.float32) / SEG
    earlier = key_at[None, :] <= query_at[:, None]
    same_seg = key_seg[None, :] == query_seg[:, None]
    seg_ids = jnp.arange(boundary.shape[1], dtype=jnp.int32)
    own_segment = query_seg[:, None] == seg_ids[None, :]
    slot_ids = seq_index * slot_count + jnp.arange(slot_count, dtype=jnp.int32)
    slot_seg = slot_ids // CSEG
    slot_at = slot_ids - slot_seg * CSEG
    tap_place = 3 * slot_at[:, None] + jnp.arange(3, dtype=jnp.int32)[None, :]
    local_row = slot_seg[:, None] * SEG + tap_place - seq_index * rows
    gather_at = jnp.where(tap_place < SEG, local_row, rows + REACH).reshape(-1)
    comp_flat = w_comp.reshape(-1, local_dim)
    shapes = [
        w_query.shape,
        w_key.shape,
        w_value.shape,
        w_out.shape,
        w_in.shape,
        w_down.shape,
        w_comp.shape,
        gains.shape,
        shifts.shape,
    ]

    def piece(matrix, index_at):
        return matrix[index_at * rows : (index_at + 1) * rows]

    def micro_step(carry, slices):
        totals, slope_total = carry
        rows_in, rows_mem, rows_comp, bound_row, link_row, cot_rows, cot_slots = slices
        bound_at = jnp.sum(jnp.where(own_segment, bound_row[None, :], 0), axis=1)
        link_at = jnp.sum(jnp.where(own_segment, link_row[None, :], 0), axis=1)
        same_doc = (key_at[None, :] >= bound_at[:, None]) | (query_at[:, None] < bound_at[:, None])
        sees_memory = (query_at < bound_at) & (link_at == 1)
        visible = same_seg & jnp.where(
            key_kind[None, :] == 0, earlier & same_doc, sees_memory[:, None]
        )
        stacked = jnp.concatenate([rows_in, rows_mem, rows_comp], axis=0).astype(jnp.float32)
        normed_f, scaled_one, inverse_one = normalize(stacked, gains[0], shifts[0])
        normed = normed_f.astype(jnp.bfloat16)
        normed_x = normed[:rows]
        queries = dot_plain(normed_x, w_query).astype(jnp.bfloat16)
        keys_own = dot_plain(normed, w_key).astype(jnp.bfloat16)
        values_own = dot_plain(normed, w_value).astype(jnp.bfloat16)
        before = shifted((keys_own, values_own), "seq", 1)
        after = shifted((keys_own[rows:], values_own[rows:], rows_mem[:REACH]), "seq", -1)

        def assemble(own_part, prev_part, next_part):
            return jnp.concatenate(
                [
                    piece(prev_part, 0),
                    piece(own_part, 0),
                    piece(prev_part, 1),
                    piece(own_part, 1),
                    piece(next_part, 0),
                    piece(prev_part, 2),
                    piece(own_part, 2),
                    piece(next_part, 1),
                ],
                axis=0,
            )

        key_heads = assemble(keys_own, before[0], after[0]).reshape(8 * rows, heads_local, HEAD)
        value_heads = assemble(values_own, before[1], after[1]).reshape(8 * rows, heads_local, HEAD)
        query_heads = queries.reshape(rows, heads_local, HEAD)

        def masked_scores():
            raw_scores = (
                jnp.einsum(
                    "qhd,khd->hqk", query_heads, key_heads, preferred_element_type=jnp.float32
                )
                * scale
            )
            raw_scores = raw_scores + slopes[:, None, None] * reach_term[None]
            return jnp.where(visible[None], raw_scores, -1e30)

        masked = masked_scores()
        row_top = jnp.max(masked, axis=-1, keepdims=True)
        log_total = row_top + jnp.log(jnp.sum(jnp.exp(masked - row_top), axis=-1, keepdims=True))
        probability = jnp.exp(masked - log_total).astype(jnp.bfloat16)
        context = (
            jnp.einsum("hqk,khd->qhd", probability, value_heads, preferred_element_type=jnp.float32)
            .reshape(rows, -1)
            .astype(jnp.bfloat16)
        )
        attended = lax.psum(dot_plain(context, w_out), "tp")
        hidden = rows_in.astype(jnp.float32) + attended
        normed_hf, scaled_two, inverse_two = normalize(hidden, gains[1], shifts[1])
        normed_h = normed_hf.astype(jnp.bfloat16)
        upper = dot_plain(normed_h, w_in)
        active_f, gelu_back = jax.vjp(
            lambda upper_in: jax.nn.gelu(upper_in, approximate=True), upper
        )
        active = active_f.astype(jnp.bfloat16)
        output = hidden + lax.psum(dot_plain(active, w_down).astype(jnp.bfloat16), "tp").astype(
            jnp.float32
        )
        extended = jnp.concatenate(
            [rows_mem, after[2], jnp.zeros((1, rows_mem.shape[1]), jnp.bfloat16)], axis=0
        )
        windows = jnp.take(extended, gather_at, axis=0).reshape(slot_count, -1)
        fresh = dot_plain(windows, comp_flat)
        grad_comp = dot_first_t(windows, cot_slots).reshape(3, -1, local_dim)
        d_windows = dot_second_t(cot_slots, comp_flat).reshape(3 * slot_count, -1)
        d_extended = (
            jnp.zeros((rows + REACH + 1, d_windows.shape[1]), jnp.float32)
            .at[gather_at]
            .add(d_windows)
        )
        grad_down = dot_first_t(active, cot_rows)
        d_upper = gelu_back(dot_second_t(cot_rows, w_down))[0].astype(jnp.bfloat16)
        grad_in = dot_first_t(normed_h, d_upper)
        d_normed_h = lax.psum(dot_second_t(d_upper, w_in), "tp")
        d_hidden_ln, gain_two, shift_two = normalize_back(
            d_normed_h, scaled_two, inverse_two, gains[1]
        )
        d_hidden = cot_rows.astype(jnp.float32) + d_hidden_ln
        d_attended = d_hidden.astype(jnp.bfloat16)
        grad_out = dot_first_t(context, d_attended)
        d_context = dot_second_t(d_attended, w_out).astype(jnp.bfloat16)
        d_context_heads = d_context.reshape(rows, heads_local, HEAD)
        masked = masked_scores()
        soft = jnp.exp(masked - log_total)
        d_soft = jnp.einsum(
            "qhd,khd->hqk", d_context_heads, value_heads, preferred_element_type=jnp.float32
        )
        d_scores = (soft * (d_soft - jnp.sum(soft * d_soft, axis=-1, keepdims=True))).astype(
            jnp.bfloat16
        )
        grad_slope = jnp.sum(d_scores.astype(jnp.float32) * reach_term[None], axis=(1, 2))
        d_queries = (
            (
                jnp.einsum("hqk,khd->qhd", d_scores, key_heads, preferred_element_type=jnp.float32)
                * scale
            )
            .reshape(rows, -1)
            .astype(jnp.bfloat16)
        )
        d_keys_all = (
            jnp.einsum(
                "hqk,qhd->khd", d_scores, query_heads, preferred_element_type=jnp.float32
            ).reshape(8 * rows, -1)
            * scale
        )
        d_values_all = jnp.einsum(
            "hqk,qhd->khd",
            soft.astype(jnp.bfloat16),
            d_context_heads,
            preferred_element_type=jnp.float32,
        ).reshape(8 * rows, -1)
        from_next = shifted(
            (
                piece(d_keys_all, 0),
                piece(d_values_all, 0),
                piece(d_keys_all, 2),
                piece(d_values_all, 2),
                piece(d_keys_all, 5),
                piece(d_values_all, 5),
            ),
            "seq",
            -1,
        )
        from_prev = (
            shifted(piece(d_keys_all, 4).astype(jnp.bfloat16), "seq", 1).astype(jnp.float32),
            shifted(piece(d_values_all, 4).astype(jnp.bfloat16), "seq", 1).astype(jnp.float32),
            shifted(piece(d_keys_all, 7).astype(jnp.bfloat16), "seq", 1).astype(jnp.float32),
            shifted(piece(d_values_all, 7).astype(jnp.bfloat16), "seq", 1).astype(jnp.float32),
            shifted(d_extended[rows : rows + REACH].astype(jnp.bfloat16), "seq", 1).astype(
                jnp.float32
            ),
        )
        d_keys = jnp.concatenate(
            [
                piece(d_keys_all, 1) + from_next[0],
                piece(d_keys_all, 3) + from_next[2] + from_prev[0],
                piece(d_keys_all, 6) + from_next[4] + from_prev[2],
            ],
            axis=0,
        ).astype(jnp.bfloat16)
        d_values = jnp.concatenate(
            [
                piece(d_values_all, 1) + from_next[1],
                piece(d_values_all, 3) + from_next[3] + from_prev[1],
                piece(d_values_all, 6) + from_next[5] + from_prev[3],
            ],
            axis=0,
        ).astype(jnp.bfloat16)
        grad_query = dot_first_t(normed_x, d_queries)
        grad_key = dot_first_t(normed, d_keys)
        grad_value = dot_first_t(normed, d_values)
        d_normed = dot_second_t(d_keys, w_key) + dot_second_t(d_values, w_value)
        d_normed = jnp.concatenate(
            [d_normed[:rows] + dot_second_t(d_queries, w_query), d_normed[rows:]], axis=0
        )
        window_part = jnp.concatenate(
            [d_extended[:REACH] + from_prev[4], d_extended[REACH:rows]], axis=0
        )
        d_normed_sum, window_sum = lax.psum((d_normed, window_part), "tp")
        d_stacked, gain_one, shift_one = normalize_back(
            d_normed_sum, scaled_one, inverse_one, gains[0]
        )
        d_input = d_hidden + d_stacked[:rows]
        d_memory = d_stacked[rows : 2 * rows] + window_sum
        d_compressed = d_stacked[2 * rows :]
        local = (
            grad_query,
            grad_key,
            grad_value,
            grad_out,
            grad_in,
            grad_down,
            grad_comp,
            jnp.stack([gain_one, gain_two]),
            jnp.stack([shift_one, shift_two]),
        )
        new_totals = tuple((running + adding for running, adding in zip(totals, local)))
        return (
            (new_totals, slope_total + grad_slope),
            (output.astype(jnp.bfloat16), d_input, d_memory, d_compressed, fresh),
        )

    start = (
        tuple((jnp.zeros(shape_one, jnp.float32) for shape_one in shapes)),
        jnp.zeros(slopes.shape, jnp.float32),
    )
    (totals, slope_total), results = lax.scan(
        micro_step, start, (inputs, memory, compressed, boundary, links, cot_out, cot_new)
    )
    summed = (
        lax.psum_scatter(totals[0], "seq", scatter_dimension=0, tiled=True),
        lax.psum_scatter(totals[1], "seq", scatter_dimension=0, tiled=True),
        lax.psum_scatter(totals[2], "seq", scatter_dimension=0, tiled=True),
        lax.psum_scatter(totals[3], "seq", scatter_dimension=1, tiled=True),
        lax.psum_scatter(totals[4], "seq", scatter_dimension=0, tiled=True),
        lax.psum_scatter(totals[5], "seq", scatter_dimension=1, tiled=True),
        lax.psum_scatter(totals[6], "seq", scatter_dimension=1, tiled=True),
        lax.psum_scatter(totals[7], "seq", scatter_dimension=1, tiled=True),
        lax.psum_scatter(totals[8], "seq", scatter_dimension=1, tiled=True),
    )
    grad_slopes = lax.psum(slope_total, "seq")
    return (
        results[0],
        results[1],
        results[2],
        results[3],
        results[4],
        summed[7],
        summed[8],
        grad_slopes,
        summed[0],
        summed[1],
        summed[2],
        summed[3],
        summed[4],
        summed[5],
        summed[6],
    )


def solution(mesh):
    in_specs = (
        P(None, "seq", None),
        P(None, "seq", None),
        P(None, "seq", None),
        P(),
        P(),
        P(),
        P(),
        P("tp"),
        P(None, "tp"),
        P(None, "tp"),
        P(None, "tp"),
        P("tp", None),
        P(None, "tp"),
        P("tp", None),
        P(None, None, "tp"),
        P(None, "seq", None),
        P(None, "seq", "tp"),
    )
    out_specs = (
        P(None, "seq", None),
        P(None, "seq", None),
        P(None, "seq", None),
        P(None, "seq", None),
        P(None, "seq", "tp"),
        P(None, "seq"),
        P(None, "seq"),
        P("tp"),
        P("seq", "tp"),
        P("seq", "tp"),
        P("seq", "tp"),
        P("tp", "seq"),
        P("seq", "tp"),
        P("tp", "seq"),
        P(None, "seq", "tp"),
    )
    return jax.shard_map(
        per_device, mesh=mesh, in_specs=in_specs, out_specs=out_specs, check_vma=False
    )
```

profile of v0, /device:TPU:0, one launch (start us, length us, event | category | flops | bytes accessed | tf_op | source)
XLA Modules:
  0.0 1682.3 jit_solution(6730223242574904582)
XLA Ops:
  11.7 1003.7 %while.43 = (s32[]{:T(128)}, f32[1024,256]{1,0:T(8,128)}, f32[1024,256]{1,0:T(8,128)}, f32[1024,256]{1,0:T(8,128)}, f32[256,1024]{1,0:T(8,128)}, /*index=5*/f32[...) while((s32[]{:T(128)}, f32[1024,256]{1,0:T(8,128)}, ...), condition=%wide.region_25.26_spmd.clone.clone.clone, body=%wide.region_0.25_spmd.clone.clone.clone.sunk | while | flops 17157980160 | bytes 980500992 | solution.py:320
  45.4 16.9 %collective-permute-done = bf16[1344,256]{1,0:T(8,128)(2,1)S(1)} collective-permute-done((bf16[1344,256]{1,0:T(8,128)(2,1)S(1)}, bf16[1344,256]{1,0:T(8,128)(2,1)S(1)}, u32[]{:S(2)}, u32[]{:S(2)}) %collective-permute-start) | collective-permute-done | bytes 688160 | tf_op jit(solution)/shard_map/while/body/eval_jaxpr/ppermute | solution.py:18
  62.4 13.4 collective-permute-done.2
  75.9 7.6 fusion.328
  100.5 5.7 scatter_custom_fusion.8
  106.9 5.0 collective-permute-start.15
  120.2 26.3 %all-reduce.8.cloned.1.call-done = f32[448,1024]{1,0:T(8,128)} async-done(((f32[448,1024]{1,0:T(8,128)}), f32[448,1024]{1,0:T(8,128)}) %all-reduce.8.cloned.1.call-update) | async-done | bytes 1835024 | tf_op jit(solution)/shard_map/while/body/eval_jaxpr/psum | solution.py:180
  170.5 33.4 %all-reduce.10.cloned.1.call-done = f32[448,1024]{1,0:T(8,128)} async-done(((f32[448,1024]{1,0:T(8,128)}), f32[448,1024]{1,0:T(8,128)}) %all-reduce.10.cloned.1.call-update) | async-done | bytes 1835024 | tf_op jit(solution)/shard_map/while/body/eval_jaxpr/psum | solution.py:207
  210.2 14.1 multiply_reduce_fusion.13
  224.6 8.9 multiply_reduce_fusion.14
  249.3 5.8 collective-permute-start.11
  258.4 41.3 %collective-permute-done.11 = bf16[448,256]{0,1:T(8,128)(2,1)S(1)} collective-permute-done((bf16[448,256]{0,1:T(8,128)(2,1)S(1)}, bf16[448,256]{0,1:T(8,128)(2,1)S(1)}, u32[]{:S(2)}, u32[]{:S(2)}) %collective-permute-start.11) | collective-permute-done | bytes 229408 | tf_op jit(solution)/shard_map/while/body/eval_jaxpr/ppermute | solution.py:18
  301.0 5.0 collective-permute-start.13
  306.9 15.1 collective-permute-done.13
  321.9 5.1 collective-permute-start.6
  329.1 5.5 collective-permute-start.8
  390.6 107.9 %all-reduce.12.cloned.1.call-done = (f32[1344,1024]{1,0:T(8,128)}, f32[448,1024]{1,0:T(8,128)}) async-done(((f32[1344,1024]{1,0:T(8,128)}, f32[448,1024]{1,0:T(8,128)}), (f32[1344,1024]{1,0:T(8,128)}, f32[448,1024]{1,0:T(8,128)})) %all-reduce.12.cloned.1.call-update) | async-done | bytes 7340048 | tf_op jit(solution)/shard_map/while/body/eval_jaxpr/psum | solution.py:292
  498.5 5.1 fusion.351
  546.1 16.9 %collective-permute-done = bf16[1344,256]{1,0:T(8,128)(2,1)S(1)} collective-permute-done((bf16[1344,256]{1,0:T(8,128)(2,1)S(1)}, bf16[1344,256]{1,0:T(8,128)(2,1)S(1)}, u32[]{:S(2)}, u32[]{:S(2)}) %collective-permute-start) | collective-permute-done | bytes 688160 | tf_op jit(solution)/shard_map/while/body/eval_jaxpr/ppermute | solution.py:18
  563.2 13.1 collective-permute-done.2
  576.4 7.6 fusion.328
  601.0 5.7 scatter_custom_fusion.8
  607.4 5.0 collective-permute-start.15
  620.7 25.8 %all-reduce.8.cloned.1.call-done = f32[448,1024]{1,0:T(8,128)} async-done(((f32[448,1024]{1,0:T(8,128)}), f32[448,1024]{1,0:T(8,128)}) %all-reduce.8.cloned.1.call-update) | async-done | bytes 1835024 | tf_op jit(solution)/shard_map/while/body/eval_jaxpr/psum | solution.py:180
  670.6 33.4 %all-reduce.10.cloned.1.call-done = f32[448,1024]{1,0:T(8,128)} async-done(((f32[448,1024]{1,0:T(8,128)}), f32[448,1024]{1,0:T(8,128)}) %all-reduce.10.cloned.1.call-update) | async-done | bytes 1835024 | tf_op jit(solution)/shard_map/while/body/eval_jaxpr/psum | solution.py:207
  710.2 14.1 multiply_reduce_fusion.13
  724.7 8.9 multiply_reduce_fusion.14
  749.5 5.8 collective-permute-start.11
  758.5 41.2 %collective-permute-done.11 = bf16[448,256]{0,1:T(8,128)(2,1)S(1)} collective-permute-done((bf16[448,256]{0,1:T(8,128)(2,1)S(1)}, bf16[448,256]{0,1:T(8,128)(2,1)S(1)}, u32[]{:S(2)}, u32[]{:S(2)}) %collective-permute-start.11) | collective-permute-done | bytes 229408 | tf_op jit(solution)/shard_map/while/body/eval_jaxpr/ppermute | solution.py:18
  801.1 5.0 collective-permute-start.13
  806.9 15.1 collective-permute-done.13
  822.0 5.1 collective-permute-start.6
  829.2 5.5 collective-permute-start.8
  868.8 5.0 select_add_fusion.8
  873.9 5.9 select_add_fusion.6
  879.8 5.7 select_add_fusion.7
  898.4 100.2 %all-reduce.12.cloned.1.call-done = (f32[1344,1024]{1,0:T(8,128)}, f32[448,1024]{1,0:T(8,128)}) async-done(((f32[1344,1024]{1,0:T(8,128)}, f32[448,1024]{1,0:T(8,128)}), (f32[1344,1024]{1,0:T(8,128)}, f32[448,1024]{1,0:T(8,128)})) %all-reduce.12.cloned.1.call-update) | async-done | bytes 7340048 | tf_op jit(solution)/shard_map/while/body/eval_jaxpr/psum | solution.py:292
  998.6 5.1 fusion.351
  1023.7 21.9 %psum.57 = f32[2]{0:T(128)} all-reduce(f32[2]{0:T(128)S(1)} %copy-done.73), channel_id=1, replica_groups=mesh['seq'=8,'tp'=4] {'seq'}, use_global_device_ids=true, to_apply=%region_28.29 | all-reduce | flops 2 | bytes 16 | tf_op jit(solution)/shard_map/psum | solution.py:334
  1045.6 35.8 %reduce-scatter.28.cloned.1.call-done = f32[128,2]{1,0:T(8,128)} async-done(((f32[1024,2]{1,0:T(8,128)}), f32[128,2]{1,0:T(8,128)}) %reduce-scatter.28.cloned.1.call-update) | async-done | bytes 1040
  1082.9 63.1 %reduce-scatter.30.cloned.1.call-done = f32[128,2]{1,0:T(8,128)} async-done(((f32[1024,2]{1,0:T(8,128)}), f32[128,2]{1,0:T(8,128)}) %reduce-scatter.30.cloned.1.call-update) | async-done | bytes 1040
  1147.5 64.9 %reduce-scatter.14.cloned.1.call-done = f32[128,256]{1,0:T(8,128)} async-done(((f32[1024,256]{1,0:T(8,128)}), f32[128,256]{1,0:T(8,128)}) %reduce-scatter.14.cloned.1.call-update) | async-done | bytes 131088 | tf_op jit(solution)/shard_map/reduce_scatter | solution.py:324
  1212.3 67.0 %reduce-scatter.16.cloned.1.call-done = f32[128,256]{1,0:T(8,128)} async-done(((f32[1024,256]{1,0:T(8,128)}), f32[128,256]{1,0:T(8,128)}) %reduce-scatter.16.cloned.1.call-update) | async-done | bytes 131088 | tf_op jit(solution)/shard_map/reduce_scatter | solution.py:325
  1279.3 66.5 %reduce-scatter.18.cloned.1.call-done = f32[128,256]{1,0:T(8,128)} async-done(((f32[1024,256]{1,0:T(8,128)}), f32[128,256]{1,0:T(8,128)}) %reduce-scatter.18.cloned.1.call-update) | async-done | bytes 131088 | tf_op jit(solution)/shard_map/reduce_scatter | solution.py:326
  1345.8 67.4 %reduce-scatter.20.cloned.1.call-done = f32[256,128]{1,0:T(8,128)} async-done(((f32[256,1024]{1,0:T(8,128)}), f32[256,128]{1,0:T(8,128)}) %reduce-scatter.20.cloned.1.call-update) | async-done | bytes 131088 | tf_op jit(solution)/shard_map/reduce_scatter | solution.py:327
  1413.2 77.7 %reduce-scatter.26.cloned.1.call-done = f32[3,128,256]{2,1,0:T(8,128)} async-done(((f32[3,1024,256]{2,1,0:T(8,128)}), f32[3,128,256]{2,1,0:T(8,128)}) %reduce-scatter.26.cloned.1.call-update) | async-done | bytes 393232 | tf_op jit(solution)/shard_map/reduce_scatter | solution.py:330
  1490.9 90.9 %reduce-scatter.22.cloned.1.call-done = f32[128,1024]{1,0:T(8,128)} async-done(((f32[1024,1024]{1,0:T(8,128)}), f32[128,1024]{1,0:T(8,128)}) %reduce-scatter.22.cloned.1.call-update) | async-done | bytes 524304 | tf_op jit(solution)/shard_map/reduce_scatter | solution.py:328
  1581.9 92.4 %reduce-scatter.24.cloned.1.call-done = f32[1024,128]{1,0:T(8,128)} async-done(((f32[1024,1024]{1,0:T(8,128)}), f32[1024,128]{1,0:T(8,128)}) %reduce-scatter.24.cloned.1.call-update) | async-done | bytes 524304 | tf_op jit(solution)/shard_map/reduce_scatter | solution.py:329
  (703 shorter events, 360.7 us)
Async XLA Ops:
  11.7 134.8 %all-reduce.8.cloned.1.call-start = ((), (), s32[]{:S(2)}) async-start(), calls=%async_computation.18 | async-start | bytes 3670016 | tf_op jit(solution)/shard_map/while/body/eval_jaxpr/psum | solution.py:180
  20.8 41.4 %collective-permute-start = (bf16[1344,256]{1,0:T(8,128)(2,1)S(1)}, bf16[1344,256]{1,0:T(8,128)(2,1)S(1)}, u32[]{:S(2)}, u32[]{:S(2)}) collective-permute-start(bf16[1344,256]{1,0:T(8,128)(2,1)S(1)} %convolution_convert_fusion.8), channel_id=1, source_target_pairs={{0,4},{4,8},{8,12},{12,16},{16,20},{20,24},{24,28},{1,5},{5,9},{9,... | collective-permute-start | bytes 2064392 | tf_op jit(solution)/shard_map/while/body/eval_jaxpr/ppermute | solution.py:18
  25.8 36.6 %collective-permute-start.1 = (bf16[896,256]{1,0:T(8,128)(2,1)S(1)}, bf16[896,256]{1,0:T(8,128)(2,1)S(1)}, u32[]{:S(2)}, u32[]{:S(2)}) collective-permute-start(bf16[896,256]{1,0:T(8,128)(2,1)S(1)} %slice.708), channel_id=1, source_target_pairs={{4,0},{8,4},{12,8},{16,12},{20,16},{24,20},{28,24},{5,1},{9,5},{13... | collective-permute-start | bytes 1376264 | tf_op jit(solution)/shard_map/while/body/eval_jaxpr/ppermute | solution.py:18
  28.0 47.8 %collective-permute-start.2 = (bf16[1344,256]{1,0:T(8,128)(2,1)S(1)}, bf16[1344,256]{1,0:T(8,128)(2,1)S(1)}, u32[]{:S(2)}, u32[]{:S(2)}) collective-permute-start(bf16[1344,256]{1,0:T(8,128)(2,1)S(1)} %convolution_convert_fusion.9), channel_id=1, source_target_pairs={{0,4},{4,8},{8,12},{12,16},{16,20},{20,24},{24,28},{1,5},{5,9},{9,... | collective-permute-start | bytes 2064392 | tf_op jit(solution)/shard_map/while/body/eval_jaxpr/ppermute | solution.py:18
  33.6 56.1 %collective-permute-start.3 = (bf16[896,256]{1,0:T(8,128)(2,1)}, bf16[896,256]{1,0:T(8,128)(2,1)}, u32[]{:S(2)}, u32[]{:S(2)}) collective-permute-start(bf16[896,256]{1,0:T(8,128)(2,1)} %slice.709), channel_id=1, source_target_pairs={{4,0},{8,4},{12,8},{16,12},{20,16},{24,20},{28,24},{5,1},{9,5},{13... | collective-permute-start | bytes 1376264 | tf_op jit(solution)/shard_map/while/body/eval_jaxpr/ppermute | solution.py:18
  35.5 80.2 %collective-permute-start.14 = (bf16[19,1024]{1,0:T(8,128)(2,1)}, bf16[19,1024]{1,0:T(8,128)(2,1)}, u32[]{:S(2)}, u32[]{:S(2)}) collective-permute-start(bf16[19,1024]{1,0:T(8,128)(2,1)} %dynamic-slice_bitcast_fusion.9), channel_id=1, source_target_pairs={{4,0},{8,4},{12,8},{16,12},{20,16},{24,20},{28,24},{5,1},{9,5},{13... | collective-permute-start | bytes 116744 | tf_op jit(solution)/shard_map/while/body/eval_jaxpr/ppermute | solution.py:18
  98.0 106.0 %all-reduce.10.cloned.1.call-start = ((), (), s32[]{:S(2)}) async-start(), calls=%async_computation.19 | async-start | bytes 3670016 | tf_op jit(solution)/shard_map/while/body/eval_jaxpr/psum | solution.py:207
  106.9 56.9 %collective-permute-start.15 = (bf16[19,1024]{1,0:T(8,128)(2,1)}, bf16[19,1024]{1,0:T(8,128)(2,1)}, u32[]{:S(2)}, u32[]{:S(2)}) collective-permute-start(bf16[19,1024]{1,0:T(8,128)(2,1)} %slice.712), channel_id=1, source_target_pairs={{0,4},{4,8},{8,12},{12,16},{16,20},{20,24},{24,28},{1,5},{5,9},{9,... | collective-permute-start | bytes 116744 | tf_op jit(solution)/shard_map/while/body/eval_jaxpr/ppermute | solution.py:18
  156.6 223.1 %all-reduce.14.cloned.1.call-start = ((), (), s32[]{:S(2)}) async-start(), calls=%async_computation.21 | async-start | bytes 1835008 | tf_op jit(solution)/shard_map/while/body/eval_jaxpr/psum | solution.py:189
  170.3 328.2 %all-reduce.12.cloned.1.call-start = ((), (), s32[]{:S(2)}) async-start(), calls=%async_computation.20 | async-start | bytes 14680064 | tf_op jit(solution)/shard_map/while/body/eval_jaxpr/psum | solution.py:292
  244.8 101.7 %collective-permute-start.4 = (f32[448,256]{0,1:T(8,128)}, f32[448,256]{0,1:T(8,128)}, u32[]{:S(2)}, u32[]{:S(2)}) collective-permute-start(f32[448,256]{0,1:T(8,128)} %bitcast.374), channel_id=1, source_target_pairs={{4,0},{8,4},{12,8},{16,12},{20,16},{24,20},{28,24},{5,1},{9,5},{13... | collective-permute-start | bytes 1376264 | tf_op jit(solution)/shard_map/while/body/eval_jaxpr/ppermute | solution.py:18
  246.1 98.5 %collective-permute-start.5 = (f32[448,256]{0,1:T(8,128)}, f32[448,256]{0,1:T(8,128)}, u32[]{:S(2)}, u32[]{:S(2)}) collective-permute-start(f32[448,256]{0,1:T(8,128)} %bitcast.375), channel_id=1, source_target_pairs={{4,0},{8,4},{12,8},{16,12},{20,16},{24,20},{28,24},{5,1},{9,5},{13... | collective-permute-start | bytes 1376264 | tf_op jit(solution)/shard_map/while/body/eval_jaxpr/ppermute | solution.py:18
  247.9 53.1 %collective-permute-start.10 = (f32[448,256]{0,1:T(8,128)S(1)}, f32[448,256]{0,1:T(8,128)S(1)}, u32[]{:S(2)}, u32[]{:S(2)}) collective-permute-start(f32[448,256]{0,1:T(8,128)S(1)} %bitcast.402), channel_id=1, source_target_pairs={{4,0},{8,4},{12,8},{16,12},{20,16},{24,20},{28,24},{5,1},{9,5},{13... | collective-permute-start | bytes 1376264 | tf_op jit(solution)/shard_map/while/body/eval_jaxpr/ppermute | solution.py:18
  249.3 50.3 %collective-permute-start.11 = (bf16[448,256]{0,1:T(8,128)(2,1)S(1)}, bf16[448,256]{0,1:T(8,128)(2,1)S(1)}, u32[]{:S(2)}, u32[]{:S(2)}) collective-permute-start(bf16[448,256]{0,1:T(8,128)(2,1)S(1)} %bitcast.404), channel_id=1, source_target_pairs={{0,4},{4,8},{8,12},{12,16},{16,20},{20,24},{24,28},{1,5},{5,9},{9,... | collective-permute-start | bytes 688136 | tf_op jit(solution)/shard_map/while/body/eval_jaxpr/ppermute | solution.py:18
  255.2 71.8 %collective-permute-start.12 = (f32[448,256]{0,1:T(8,128)S(1)}, f32[448,256]{0,1:T(8,128)S(1)}, u32[]{:S(2)}, u32[]{:S(2)}) collective-permute-start(f32[448,256]{0,1:T(8,128)S(1)} %bitcast.401), channel_id=1, source_target_pairs={{4,0},{8,4},{12,8},{16,12},{20,16},{24,20},{28,24},{5,1},{9,5},{13... | collective-permute-start | bytes 1376264 | tf_op jit(solution)/shard_map/while/body/eval_jaxpr/ppermute | solution.py:18
  299.7 29.5 %collective-permute-start.9 = (f32[448,256]{0,1:T(8,128)S(1)}, f32[448,256]{0,1:T(8,128)S(1)}, u32[]{:S(2)}, u32[]{:S(2)}) collective-permute-start(f32[448,256]{0,1:T(8,128)S(1)} %bitcast.400), channel_id=1, source_target_pairs={{4,0},{8,4},{12,8},{16,12},{20,16},{24,20},{28,24},{5,1},{9,5},{13... | collective-permute-start | bytes 1376264 | tf_op jit(solution)/shard_map/while/body/eval_jaxpr/ppermute | solution.py:18
  301.0 20.9 %collective-permute-start.13 = (bf16[448,256]{0,1:T(8,128)(2,1)S(1)}, bf16[448,256]{0,1:T(8,128)(2,1)S(1)}, u32[]{:S(2)}, u32[]{:S(2)}) collective-permute-start(bf16[448,256]{0,1:T(8,128)(2,1)S(1)} %bitcast.403), channel_id=1, source_target_pairs={{0,4},{4,8},{8,12},{12,16},{16,20},{20,24},{24,28},{1,5},{5,9},{9,... | collective-permute-start | bytes 688136 | tf_op jit(solution)/shard_map/while/body/eval_jaxpr/ppermute | solution.py:18
  321.9 22.6 %collective-permute-start.6 = (bf16[448,256]{0,1:T(8,128)(2,1)}, bf16[448,256]{0,1:T(8,128)(2,1)}, u32[]{:S(2)}, u32[]{:S(2)}) collective-permute-start(bf16[448,256]{0,1:T(8,128)(2,1)} %bitcast.376), channel_id=1, source_target_pairs={{0,4},{4,8},{8,12},{12,16},{16,20},{20,24},{24,28},{1,5},{5,9},{9,... | collective-permute-start | bytes 688136 | tf_op jit(solution)/shard_map/while/body/eval_jaxpr/ppermute | solution.py:18
  327.0 22.2 %collective-permute-start.7 = (f32[448,256]{0,1:T(8,128)}, f32[448,256]{0,1:T(8,128)}, u32[]{:S(2)}, u32[]{:S(2)}) collective-permute-start(f32[448,256]{0,1:T(8,128)} %bitcast.377), channel_id=1, source_target_pairs={{4,0},{8,4},{12,8},{16,12},{20,16},{24,20},{28,24},{5,1},{9,5},{13... | collective-permute-start | bytes 1376264 | tf_op jit(solution)/shard_map/while/body/eval_jaxpr/ppermute | solution.py:18
  329.1 20.1 %collective-permute-start.8 = (bf16[448,256]{0,1:T(8,128)(2,1)}, bf16[448,256]{0,1:T(8,128)(2,1)}, u32[]{:S(2)}, u32[]{:S(2)}) collective-permute-start(bf16[448,256]{0,1:T(8,128)(2,1)} %bitcast.378), channel_id=1, source_target_pairs={{0,4},{4,8},{8,12},{12,16},{16,20},{20,24},{24,28},{1,5},{5,9},{9,... | collective-permute-start | bytes 688136 | tf_op jit(solution)/shard_map/while/body/eval_jaxpr/ppermute | solution.py:18
  513.9 132.6 %all-reduce.8.cloned.1.call-start = ((), (), s32[]{:S(2)}) async-start(), calls=%async_computation.18 | async-start | bytes 3670016 | tf_op jit(solution)/shard_map/while/body/eval_jaxpr/psum | solution.py:180
  523.1 40.0 %collective-permute-start = (bf16[1344,256]{1,0:T(8,128)(2,1)S(1)}, bf16[1344,256]{1,0:T(8,128)(2,1)S(1)}, u32[]{:S(2)}, u32[]{:S(2)}) collective-permute-start(bf16[1344,256]{1,0:T(8,128)(2,1)S(1)} %convolution_convert_fusion.8), channel_id=1, source_target_pairs={{0,4},{4,8},{8,12},{12,16},{16,20},{20,24},{24,28},{1,5},{5,9},{9,... | collective-permute-start | bytes 2064392 | tf_op jit(solution)/shard_map/while/body/eval_jaxpr/ppermute | solution.py:18
  526.5 36.6 %collective-permute-start.1 = (bf16[896,256]{1,0:T(8,128)(2,1)S(1)}, bf16[896,256]{1,0:T(8,128)(2,1)S(1)}, u32[]{:S(2)}, u32[]{:S(2)}) collective-permute-start(bf16[896,256]{1,0:T(8,128)(2,1)S(1)} %slice.708), channel_id=1, source_target_pairs={{4,0},{8,4},{12,8},{16,12},{20,16},{24,20},{28,24},{5,1},{9,5},{13... | collective-permute-start | bytes 1376264 | tf_op jit(solution)/shard_map/while/body/eval_jaxpr/ppermute | solution.py:18
  528.8 47.5 %collective-permute-start.2 = (bf16[1344,256]{1,0:T(8,128)(2,1)S(1)}, bf16[1344,256]{1,0:T(8,128)(2,1)S(1)}, u32[]{:S(2)}, u32[]{:S(2)}) collective-permute-start(bf16[1344,256]{1,0:T(8,128)(2,1)S(1)} %convolution_convert_fusion.9), channel_id=1, source_target_pairs={{0,4},{4,8},{8,12},{12,16},{16,20},{20,24},{24,28},{1,5},{5,9},{9,... | collective-permute-start | bytes 2064392 | tf_op jit(solution)/shard_map/while/body/eval_jaxpr/ppermute | solution.py:18
  534.3 55.8 %collective-permute-start.3 = (bf16[896,256]{1,0:T(8,128)(2,1)}, bf16[896,256]{1,0:T(8,128)(2,1)}, u32[]{:S(2)}, u32[]{:S(2)}) collective-permute-start(bf16[896,256]{1,0:T(8,128)(2,1)} %slice.709), channel_id=1, source_target_pairs={{4,0},{8,4},{12,8},{16,12},{20,16},{24,20},{28,24},{5,1},{9,5},{13... | collective-permute-start | bytes 1376264 | tf_op jit(solution)/shard_map/while/body/eval_jaxpr/ppermute | solution.py:18
  536.3 79.9 %collective-permute-start.14 = (bf16[19,1024]{1,0:T(8,128)(2,1)}, bf16[19,1024]{1,0:T(8,128)(2,1)}, u32[]{:S(2)}, u32[]{:S(2)}) collective-permute-start(bf16[19,1024]{1,0:T(8,128)(2,1)} %dynamic-slice_bitcast_fusion.9), channel_id=1, source_target_pairs={{4,0},{8,4},{12,8},{16,12},{20,16},{24,20},{28,24},{5,1},{9,5},{13... | collective-permute-start | bytes 116744 | tf_op jit(solution)/shard_map/while/body/eval_jaxpr/ppermute | solution.py:18
  598.5 105.5 %all-reduce.10.cloned.1.call-start = ((), (), s32[]{:S(2)}) async-start(), calls=%async_computation.19 | async-start | bytes 3670016 | tf_op jit(solution)/shard_map/while/body/eval_jaxpr/psum | solution.py:207
  607.4 56.5 %collective-permute-start.15 = (bf16[19,1024]{1,0:T(8,128)(2,1)}, bf16[19,1024]{1,0:T(8,128)(2,1)}, u32[]{:S(2)}, u32[]{:S(2)}) collective-permute-start(bf16[19,1024]{1,0:T(8,128)(2,1)} %slice.712), channel_id=1, source_target_pairs={{0,4},{4,8},{8,12},{12,16},{16,20},{20,24},{24,28},{1,5},{5,9},{9,... | collective-permute-start | bytes 116744 | tf_op jit(solution)/shard_map/while/body/eval_jaxpr/ppermute | solution.py:18
  656.7 228.8 %all-reduce.14.cloned.1.call-start = ((), (), s32[]{:S(2)}) async-start(), calls=%async_computation.21 | async-start | bytes 1835008 | tf_op jit(solution)/shard_map/while/body/eval_jaxpr/psum | solution.py:189
  670.4 328.2 %all-reduce.12.cloned.1.call-start = ((), (), s32[]{:S(2)}) async-start(), calls=%async_computation.20 | async-start | bytes 14680064 | tf_op jit(solution)/shard_map/while/body/eval_jaxpr/psum | solution.py:292
  744.9 101.6 %collective-permute-start.4 = (f32[448,256]{0,1:T(8,128)}, f32[448,256]{0,1:T(8,128)}, u32[]{:S(2)}, u32[]{:S(2)}) collective-permute-start(f32[448,256]{0,1:T(8,128)} %bitcast.374), channel_id=1, source_target_pairs={{4,0},{8,4},{12,8},{16,12},{20,16},{24,20},{28,24},{5,1},{9,5},{13... | collective-permute-start | bytes 1376264 | tf_op jit(solution)/shard_map/while/body/eval_jaxpr/ppermute | solution.py:18
  746.2 98.4 %collective-permute-start.5 = (f32[448,256]{0,1:T(8,128)}, f32[448,256]{0,1:T(8,128)}, u32[]{:S(2)}, u32[]{:S(2)}) collective-permute-start(f32[448,256]{0,1:T(8,128)} %bitcast.375), channel_id=1, source_target_pairs={{4,0},{8,4},{12,8},{16,12},{20,16},{24,20},{28,24},{5,1},{9,5},{13... | collective-permute-start | bytes 1376264 | tf_op jit(solution)/shard_map/while/body/eval_jaxpr/ppermute | solution.py:18
  748.0 53.0 %collective-permute-start.10 = (f32[448,256]{0,1:T(8,128)S(1)}, f32[448,256]{0,1:T(8,128)S(1)}, u32[]{:S(2)}, u32[]{:S(2)}) collective-permute-start(f32[448,256]{0,1:T(8,128)S(1)} %bitcast.402), channel_id=1, source_target_pairs={{4,0},{8,4},{12,8},{16,12},{20,16},{24,20},{28,24},{5,1},{9,5},{13... | collective-permute-start | bytes 1376264 | tf_op jit(solution)/shard_map/while/body/eval_jaxpr/ppermute | solution.py:18
  749.5 50.3 %collective-permute-start.11 = (bf16[448,256]{0,1:T(8,128)(2,1)S(1)}, bf16[448,256]{0,1:T(8,128)(2,1)S(1)}, u32[]{:S(2)}, u32[]{:S(2)}) collective-permute-start(bf16[448,256]{0,1:T(8,128)(2,1)S(1)} %bitcast.404), channel_id=1, source_target_pairs={{0,4},{4,8},{8,12},{12,16},{16,20},{20,24},{24,28},{1,5},{5,9},{9,... | collective-permute-start | bytes 688136 | tf_op jit(solution)/shard_map/while/body/eval_jaxpr/ppermute | solution.py:18
  755.3 71.8 %collective-permute-start.12 = (f32[448,256]{0,1:T(8,128)S(1)}, f32[448,256]{0,1:T(8,128)S(1)}, u32[]{:S(2)}, u32[]{:S(2)}) collective-permute-start(f32[448,256]{0,1:T(8,128)S(1)} %bitcast.401), channel_id=1, source_target_pairs={{4,0},{8,4},{12,8},{16,12},{20,16},{24,20},{28,24},{5,1},{9,5},{13... | collective-permute-start | bytes 1376264 | tf_op jit(solution)/shard_map/while/body/eval_jaxpr/ppermute | solution.py:18
  799.8 29.5 %collective-permute-start.9 = (f32[448,256]{0,1:T(8,128)S(1)}, f32[448,256]{0,1:T(8,128)S(1)}, u32[]{:S(2)}, u32[]{:S(2)}) collective-permute-start(f32[448,256]{0,1:T(8,128)S(1)} %bitcast.400), channel_id=1, source_target_pairs={{4,0},{8,4},{12,8},{16,12},{20,16},{24,20},{28,24},{5,1},{9,5},{13... | collective-permute-start | bytes 1376264 | tf_op jit(solution)/shard_map/while/body/eval_jaxpr/ppermute | solution.py:18
  801.1 20.9 %collective-permute-start.13 = (bf16[448,256]{0,1:T(8,128)(2,1)S(1)}, bf16[448,256]{0,1:T(8,128)(2,1)S(1)}, u32[]{:S(2)}, u32[]{:S(2)}) collective-permute-start(bf16[448,256]{0,1:T(8,128)(2,1)S(1)} %bitcast.403), channel_id=1, source_target_pairs={{0,4},{4,8},{8,12},{12,16},{16,20},{20,24},{24,28},{1,5},{5,9},{9,... | collective-permute-start | bytes 688136 | tf_op jit(solution)/shard_map/while/body/eval_jaxpr/ppermute | solution.py:18
  822.0 22.6 %collective-permute-start.6 = (bf16[448,256]{0,1:T(8,128)(2,1)}, bf16[448,256]{0,1:T(8,128)(2,1)}, u32[]{:S(2)}, u32[]{:S(2)}) collective-permute-start(bf16[448,256]{0,1:T(8,128)(2,1)} %bitcast.376), channel_id=1, source_target_pairs={{0,4},{4,8},{8,12},{12,16},{16,20},{20,24},{24,28},{1,5},{5,9},{9,... | collective-permute-start | bytes 688136 | tf_op jit(solution)/shard_map/while/body/eval_jaxpr/ppermute | solution.py:18
  827.1 22.2 %collective-permute-start.7 = (f32[448,256]{0,1:T(8,128)}, f32[448,256]{0,1:T(8,128)}, u32[]{:S(2)}, u32[]{:S(2)}) collective-permute-start(f32[448,256]{0,1:T(8,128)} %bitcast.377), channel_id=1, source_target_pairs={{4,0},{8,4},{12,8},{16,12},{20,16},{24,20},{28,24},{5,1},{9,5},{13... | collective-permute-start | bytes 1376264 | tf_op jit(solution)/shard_map/while/body/eval_jaxpr/ppermute | solution.py:18
  1015.3 66.1 %reduce-scatter.28.cloned.1.call-start = ((), (), s32[]{:S(2)}) async-start(), calls=%async_computation.16 | async-start | bytes 589824
  1017.1 128.9 %reduce-scatter.30.cloned.1.call-start = ((), (), s32[]{:S(2)}) async-start(), calls=%async_computation.17 | async-start | bytes 589824
  1018.9 193.4 %reduce-scatter.14.cloned.1.call-start = ((), (), s32[]{:S(2)}) async-start(), calls=%async_computation.9 | async-start | bytes 1179648 | tf_op jit(solution)/shard_map/reduce_scatter | solution.py:324
  1019.5 259.8 %reduce-scatter.16.cloned.1.call-start = ((), (), s32[]{:S(2)}) async-start(), calls=%async_computation.10 | async-start | bytes 1179648 | tf_op jit(solution)/shard_map/reduce_scatter | solution.py:325
  1020.3 325.5 %reduce-scatter.18.cloned.1.call-start = ((), (), s32[]{:S(2)}) async-start(), calls=%async_computation.11 | async-start | bytes 1179648 | tf_op jit(solution)/shard_map/reduce_scatter | solution.py:326
  1021.0 392.2 %reduce-scatter.20.cloned.1.call-start = ((), (), s32[]{:S(2)}) async-start(), calls=%async_computation.12 | async-start | bytes 1179648 | tf_op jit(solution)/shard_map/reduce_scatter | solution.py:327
  1021.8 469.2 %reduce-scatter.26.cloned.1.call-start = ((), (), s32[]{:S(2)}) async-start(), calls=%async_computation.15 | async-start | bytes 3538944 | tf_op jit(solution)/shard_map/reduce_scatter | solution.py:330
  1022.3 559.5 %reduce-scatter.22.cloned.1.call-start = ((), (), s32[]{:S(2)}) async-start(), calls=%async_computation.13 | async-start | bytes 4718592 | tf_op jit(solution)/shard_map/reduce_scatter | solution.py:328
  1022.9 651.4 %reduce-scatter.24.cloned.1.call-start = ((), (), s32[]{:S(2)}) async-start(), calls=%async_computation.14 | async-start | bytes 4718592 | tf_op jit(solution)/shard_map/reduce_scatter | solution.py:329
  (188 other events, 1695.8 us)
Sparse Core Ops, SparseCore 0:
  98.1 48.3 all-reduce.7
  156.7 47.1 all-reduce.9
  206.4 35.3 all-reduce.13
  361.4 137.0 all-reduce.11
  598.6 47.8 all-reduce.7
  656.8 47.1 all-reduce.9
  706.4 35.3 all-reduce.13
  861.4 137.0 all-reduce.11
Sparse Core Ops, SparseCore 1:
  1019.1 62.2 reduce-scatter.27
  1085.0 61.0 reduce-scatter.29
  1149.9 62.4 reduce-scatter.13
  1216.7 62.5 reduce-scatter.15
  1283.3 62.4 reduce-scatter.17
  1350.2 63.0 reduce-scatter.19
  1417.3 73.6 reduce-scatter.25
  1495.0 86.8 reduce-scatter.21
  1586.4 87.9 reduce-scatter.23
where the time goes:
time: 1690 us; the launch traced here: 1680 us
  waiting for transfers between devices  1140 us (67%)
  matrix products  155 us (9%)
  other arithmetic  139 us (8%)
  local copies, waits for them, and re-layouts  110 us (7%)
  starting transfers between devices  95.9 us (6%)
  blocking collectives  21.9 us (1%)
    psum x2, waiting for transfers between devices, micro_step(): d_normed_sum, window_sum = lax.psum((d_normed, window_part), 'tp')  208 us
    ppermute x32, waiting for transfers between devices, shifted(): return lax.ppermute(block, axis, route)  181 us
    unnamed x11, waiting for transfers between devices  103 us
    ppermute x32, starting transfers between devices, shifted(): return lax.ppermute(block, axis, route)  94 us
    reduce_scatter x1, waiting for transfers between devices, per_device(): lax.psum_scatter(totals[5], 'seq', scatter_dimension=1, tiled=True)  92.4 us
    reduce_scatter x1, waiting for transfers between devices, per_device(): lax.psum_scatter(totals[4], 'seq', scatter_dimension=0, tiled=True)  90.9 us
    reduce_scatter x1, waiting for transfers between devices, per_device(): lax.psum_scatter(totals[6], 'seq', scatter_dimension=1, tiled=True)  77.7 us
    reduce_scatter x1, waiting for transfers between devices, per_device(): lax.psum_scatter(totals[3], 'seq', scatter_dimension=1, tiled=True)  67.4 us
  transfers between devices with their start and end apart: 49, of which 27 were waited for; matrix products, arithmetic and copies ran while one was open for 20% of the time, Pallas kernels for 0%

commit v1 on v0

--- a/solution.py
+++ b/solution.py
@@ -1,6 +1,10 @@
+import functools
+
 import jax
 import jax.numpy as jnp
 from jax import lax
+from jax.experimental import pallas as pl
+from jax.experimental.pallas import tpu as pltpu
 from jax.sharding import PartitionSpec as P
 
 HEAD = 128
@@ -47,6 +51,106 @@
     second_mean = jnp.mean(weighted * scaled, axis=-1, keepdims=True)
     grad_input = inverse * (weighted - first_mean - scaled * second_mean)
     return (grad_input, jnp.sum(grad_rows * scaled, axis=0), jnp.sum(grad_rows, axis=0))
+
+
+MESH = pl.DeviceIdType.MESH
+
+
+def bit_view(array, count):
+    bits = count.bit_length() - 1
+    return array.reshape((2,) * bits + (array.shape[0] // count, array.shape[1]))
+
+
+def halving_kernel(count, width, grads, total, landed, kept, send_sem, recv_sem):
+    bits = count.bit_length() - 1
+    me = lax.axis_index("seq")
+    tp_me = lax.axis_index("tp")
+    mine = [lax.rem(lax.div(me, 1 << b), 2) for b in range(bits)]
+    chunks = grads.shape[-1] // width
+
+    def partner(bit):
+        return (me + (1 - 2 * mine[bit]) * (1 << bit), tp_me)
+
+    barrier = pltpu.get_barrier_semaphore()
+    for bit in range(bits):
+        pl.semaphore_signal(barrier, inc=1, device_id=partner(bit), device_id_type=MESH)
+    pl.semaphore_wait(barrier, bits)
+
+    def order(chunk):
+        return [(i + chunk % 2) % bits for i in range(bits)]
+
+    def where(left, bit, own):
+        return tuple(
+            (mine[b] if own else 1 - mine[b]) if b == bit else slice(None) for b in left
+        )
+
+    def cols(chunk):
+        return pl.ds(chunk * width, width)
+
+    def source(chunk, step):
+        return grads if step == 0 else kept[step - 1]
+
+    def copy(chunk, step):
+        plan = order(chunk)
+        left = [b for b in reversed(range(bits)) if b not in plan[:step]]
+        index = where(left, plan[step], False) + (slice(None), cols(chunk))
+        return pltpu.make_async_remote_copy(
+            src_ref=source(chunk, step).at[index],
+            dst_ref=landed[step].at[(slice(None),) * (bits - step) + (cols(chunk),)],
+            send_sem=send_sem.at[step, chunk],
+            recv_sem=recv_sem.at[step, chunk],
+            device_id=partner(plan[step]),
+            device_id_type=MESH,
+        )
+
+    def finish(chunk, step):
+        copy(chunk, step).wait()
+        plan = order(chunk)
+        left = [b for b in reversed(range(bits)) if b not in plan[:step]]
+        index = where(left, plan[step], True) + (slice(None), cols(chunk))
+        mine_part = source(chunk, step)[index].astype(jnp.float32)
+        came = landed[step][(slice(None),) * (bits - step) + (cols(chunk),)]
+        added = mine_part + came.astype(jnp.float32)
+        if step == bits - 1:
+            total[:, cols(chunk)] = added
+        else:
+            kept[step][(slice(None),) * (bits - step) + (cols(chunk),)] = added.astype(jnp.bfloat16)
+            copy(chunk, step + 1).start()
+
+    group = 2
+    for turn in range(chunks // group + bits):
+        for step in reversed(range(bits)):
+            for at in range(group):
+                chunk = (turn - step - 1) * group + at
+                if 0 <= chunk < chunks:
+                    finish(chunk, step)
+        for at in range(group):
+            chunk = turn * group + at
+            if chunk < chunks:
+                copy(chunk, 0).start()
+
+
+def reduce_over_seq(grads):
+    count = lax.axis_size("seq")
+    bits = count.bit_length() - 1
+    rows, columns = grads.shape[0] // count, grads.shape[1]
+    width = 256
+    chunks = columns // width
+    return pl.pallas_call(
+        functools.partial(halving_kernel, count, width),
+        out_shape=jax.ShapeDtypeStruct((rows, columns), jnp.float32),
+        in_specs=[pl.BlockSpec(memory_space=pltpu.VMEM)],
+        out_specs=pl.BlockSpec(memory_space=pltpu.VMEM),
+        scratch_shapes=[
+            [pltpu.VMEM((2,) * (bits - 1 - i) + (rows, columns), jnp.bfloat16) for i in range(bits)],
+            [pltpu.VMEM((2,) * (bits - 1 - i) + (rows, columns), jnp.bfloat16) for i in range(bits - 1)],
+            pltpu.SemaphoreType.DMA((bits, chunks)),
+            pltpu.SemaphoreType.DMA((bits, chunks)),
+        ],
+        compiler_params=pltpu.CompilerParams(
+            collective_id=1, has_side_effects=True, vmem_limit_bytes=50 << 20
+        ),
+    )(bit_view(grads, count))
 
 
 def per_device(
@@ -320,16 +424,37 @@
     (totals, slope_total), results = lax.scan(
         micro_step, start, (inputs, memory, compressed, boundary, links, cot_out, cot_new)
     )
+    pieces = [
+        totals[0],
+        totals[1],
+        totals[2],
+        totals[3].T,
+        totals[4],
+        totals[5].T,
+        totals[6][0],
+        totals[6][1],
+        totals[6][2],
+        jnp.pad(jnp.concatenate([totals[7], totals[8]], axis=0).T, ((0, 0), (0, 252))),
+    ]
+    mixed = reduce_over_seq(
+        jnp.concatenate([matrix.astype(jnp.bfloat16) for matrix in pieces], axis=1)
+    )
+    out_rows = []
+    at = 0
+    for matrix in pieces:
+        out_rows.append(mixed[:, at : at + matrix.shape[1]])
+        at += matrix.shape[1]
+    vectors = out_rows[9][:, :4].T
     summed = (
-        lax.psum_scatter(totals[0], "seq", scatter_dimension=0, tiled=True),
-        lax.psum_scatter(totals[1], "seq", scatter_dimension=0, tiled=True),
-        lax.psum_scatter(totals[2], "seq", scatter_dimension=0, tiled=True),
-        lax.psum_scatter(totals[3], "seq", scatter_dimension=1, tiled=True),
-        lax.psum_scatter(totals[4], "seq", scatter_dimension=0, tiled=True),
-        lax.psum_scatter(totals[5], "seq", scatter_dimension=1, tiled=True),
-        lax.psum_scatter(totals[6], "seq", scatter_dimension=1, tiled=True),
-        lax.psum_scatter(totals[7], "seq", scatter_dimension=1, tiled=True),
-        lax.psum_scatter(totals[8], "seq", scatter_dimension=1, tiled=True),
+        out_rows[0],
+        out_rows[1],
+        out_rows[2],
+        out_rows[3].T,
+        out_rows[4],
+        out_rows[5].T,
+        jnp.stack(out_rows[6:9]),
+        vectors[:2],
+        vectors[2:],
     )
     grad_slopes = lax.psum(slope_total, "seq")
     return (

time: 1690 us -> 1200 us (0.71)
  waiting for transfers between devices: 1140 us -> 507 us
  Pallas kernels: 0 us -> 115 us
  local copies, waits for them, and re-layouts: 110 us -> 134 us
    reduce_scatter x7 -> x0, waiting for transfers between devices: 527 us -> none  [the longest x1 92.4 us: per_device(): lax.psum_scatter(totals[5], 'seq', scatter_dimension=1, tiled=True)]
    pallas_call x0 -> x1, Pallas kernels: none -> 115 us  [reduce_over_seq(): pl.pallas_call(functools.partial(halving_kernel, count, width), out_shape...]
    unnamed x11 -> x0, waiting for transfers between devices: 103 us -> none
    while x404 -> x400, local copies, waits for them, and re-layouts: 39.1 us -> 44.9 us
  transfers between devices with their start and end apart: 49 -> 40, of which waited for: 27 -> 18; matrix products, arithmetic and copies ran while one was open for 20% -> 28% of each run, Pallas kernels for 0% -> 0%
where the time goes in v1:
time: 1200 us
  waiting for transfers between devices  507 us (42%)
  matrix products  155 us (13%)
  other arithmetic  146 us (12%)
  local copies, waits for them, and re-layouts  134 us (11%)
  Pallas kernels  115 us (10%)
  starting transfers between devices  95.9 us (8%)
  blocking collectives  20.3 us (2%)
  between operations  14.6 us (1%)
    psum x2, waiting for transfers between devices, micro_step(): d_normed_sum, window_sum = lax.psum((d_normed, window_part), 'tp')  209 us
    ppermute x32, waiting for transfers between devices, shifted(): return lax.ppermute(block, axis, route)  181 us
    pallas_call x1, Pallas kernels, reduce_over_seq(): pl.pallas_call(functools.partial(halving_kernel, count, width), out_shape...  115 us
    ppermute x32, starting transfers between devices, shifted(): return lax.ppermute(block, axis, route)  94.5 us
    psum x2, waiting for transfers between devices, micro_step(): d_normed_h = lax.psum(dot_second_t(d_upper, w_in), 'tp')  66.3 us
    psum x2, waiting for transfers between devices, micro_step(): attended = lax.psum(dot_plain(context, w_out), 'tp')  51.2 us
    dot_general x14, matrix products, dot_first_t(): lax.dot_general(matrix_a, matrix_b, (((0,), (0,)), ((), ())), preferred_e...  41.3 us
    while x396, local copies, waits for them, and re-layouts  38.4 us
  transfers between devices with their start and end apart: 40, of which 18 were waited for; matrix products, arithmetic and copies ran while one was open for 28% of the time, Pallas kernels for 0%

profile of v1, /device:TPU:0, one launch (start us, length us, event | category | flops | bytes accessed | tf_op | source)
XLA Modules:
  0.0 1196.8 jit_solution(3183312752630314318)
XLA Ops:
  10.8 1006.8 %while.43 = (s32[]{:T(128)}, f32[1024,256]{1,0:T(8,128)}, f32[1024,256]{1,0:T(8,128)}, f32[1024,256]{1,0:T(8,128)}, f32[256,1024]{1,0:T(8,128)}, /*index=5*/f32[...) while((s32[]{:T(128)}, f32[1024,256]{1,0:T(8,128)}, ...), condition=%wide.region_25.26_spmd.clone.clone.clone, body=%wide.region_0.25_spmd.clone.clone.clone.sunk | while | flops 17157980160 | bytes 980496000 | solution.py:424
  20.0 4.9 collective-permute-start
  27.2 4.7 collective-permute-start.2
  44.8 16.6 %collective-permute-done = bf16[1344,256]{1,0:T(8,128)(2,1)S(1)} collective-permute-done((bf16[1344,256]{1,0:T(8,128)(2,1)S(1)}, bf16[1344,256]{1,0:T(8,128)(2,1)S(1)}, u32[]{:S(2)}, u32[]{:S(2)}) %collective-permute-start) | collective-permute-done | bytes 688160 | tf_op jit(solution)/shard_map/while/body/eval_jaxpr/ppermute | solution.py:22
  61.6 13.4 %collective-permute-done.2 = bf16[1344,256]{1,0:T(8,128)(2,1)S(1)} collective-permute-done((bf16[1344,256]{1,0:T(8,128)(2,1)S(1)}, bf16[1344,256]{1,0:T(8,128)(2,1)S(1)}, u32[]{:S(2)}, u32[]{:S(2)}) %collective-permute-start.2) | collective-permute-done | bytes 688160 | tf_op jit(solution)/shard_map/while/body/eval_jaxpr/ppermute | solution.py:22
  75.1 7.6 fusion.329
  99.4 5.7 scatter_custom_fusion.8
  105.8 5.0 collective-permute-start.15
  119.8 25.8 %all-reduce.9.cloned.1.call-done = f32[448,1024]{1,0:T(8,128)} async-done(((f32[448,1024]{1,0:T(8,128)}), f32[448,1024]{1,0:T(8,128)}) %all-reduce.9.cloned.1.call-update) | async-done | bytes 1835024 | tf_op jit(solution)/shard_map/while/body/eval_jaxpr/psum | solution.py:284
  169.9 33.2 %all-reduce.11.cloned.1.call-done = f32[448,1024]{1,0:T(8,128)} async-done(((f32[448,1024]{1,0:T(8,128)}), f32[448,1024]{1,0:T(8,128)}) %all-reduce.11.cloned.1.call-update) | async-done | bytes 1835024 | tf_op jit(solution)/shard_map/while/body/eval_jaxpr/psum | solution.py:311
  209.3 14.1 %multiply_reduce_fusion.13 = (f32[2,448]{1,0:T(2,128)S(1)}, f32[2,448,3584]{2,1,0:T(8,128)}) fusion(f32[2,448,3584]{2,1,0:T(8,128)} %copy-done, f32[2,448]{1,0:T(2,128)S(1)} %log_add_fusion.2, bf16[56,2,8,128]{3,2,1,0:T(8,128)(2,1)S(1)} %fusion.336, bf16[3584,256]{1,0:T(8,128)(2,1)} %copy-done.9), kind=kOutput, calls=%fused_computation.10.clone.1 | convolution fusion | flops 831716480 | bytes 27761664 | tf_op jit(solution)/shard_map/while/body/eval_jaxpr/qhd,khd->hqk/dot_general | solution.py:322
  223.8 9.0 multiply_reduce_fusion.14
  248.6 5.8 collective-permute-start.11
  257.6 41.3 %collective-permute-done.11 = bf16[448,256]{0,1:T(8,128)(2,1)S(1)} collective-permute-done((bf16[448,256]{0,1:T(8,128)(2,1)S(1)}, bf16[448,256]{0,1:T(8,128)(2,1)S(1)}, u32[]{:S(2)}, u32[]{:S(2)}) %collective-permute-start.11) | collective-permute-done | bytes 229408 | tf_op jit(solution)/shard_map/while/body/eval_jaxpr/ppermute | solution.py:22
  300.2 5.0 collective-permute-start.13
  306.1 15.1 %collective-permute-done.13 = bf16[448,256]{0,1:T(8,128)(2,1)S(1)} collective-permute-done((bf16[448,256]{0,1:T(8,128)(2,1)S(1)}, bf16[448,256]{0,1:T(8,128)(2,1)S(1)}, u32[]{:S(2)}, u32[]{:S(2)}) %collective-permute-start.13) | collective-permute-done | bytes 229408 | tf_op jit(solution)/shard_map/while/body/eval_jaxpr/ppermute | solution.py:22
  321.1 5.1 collective-permute-start.6
  328.3 5.4 collective-permute-start.8
  336.0 4.5 fusion.350
  363.6 4.4 dynamic_update_slice.57
  389.2 108.6 %all-reduce.13.cloned.1.call-done = (f32[1344,1024]{1,0:T(8,128)}, f32[448,1024]{1,0:T(8,128)}) async-done(((f32[1344,1024]{1,0:T(8,128)}, f32[448,1024]{1,0:T(8,128)}), (f32[1344,1024]{1,0:T(8,128)}, f32[448,1024]{1,0:T(8,128)})) %all-reduce.13.cloned.1.call-update) | async-done | bytes 7340048 | tf_op jit(solution)/shard_map/while/body/eval_jaxpr/psum | solution.py:396
  497.7 5.1 fusion.352
  527.8 4.7 collective-permute-start.2
  545.4 16.6 %collective-permute-done = bf16[1344,256]{1,0:T(8,128)(2,1)S(1)} collective-permute-done((bf16[1344,256]{1,0:T(8,128)(2,1)S(1)}, bf16[1344,256]{1,0:T(8,128)(2,1)S(1)}, u32[]{:S(2)}, u32[]{:S(2)}) %collective-permute-start) | collective-permute-done | bytes 688160 | tf_op jit(solution)/shard_map/while/body/eval_jaxpr/ppermute | solution.py:22
  562.2 13.1 %collective-permute-done.2 = bf16[1344,256]{1,0:T(8,128)(2,1)S(1)} collective-permute-done((bf16[1344,256]{1,0:T(8,128)(2,1)S(1)}, bf16[1344,256]{1,0:T(8,128)(2,1)S(1)}, u32[]{:S(2)}, u32[]{:S(2)}) %collective-permute-start.2) | collective-permute-done | bytes 688160 | tf_op jit(solution)/shard_map/while/body/eval_jaxpr/ppermute | solution.py:22
  575.4 7.6 fusion.329
  599.7 5.7 scatter_custom_fusion.8
  606.1 5.0 collective-permute-start.15
  620.1 25.4 %all-reduce.9.cloned.1.call-done = f32[448,1024]{1,0:T(8,128)} async-done(((f32[448,1024]{1,0:T(8,128)}), f32[448,1024]{1,0:T(8,128)}) %all-reduce.9.cloned.1.call-update) | async-done | bytes 1835024 | tf_op jit(solution)/shard_map/while/body/eval_jaxpr/psum | solution.py:284
  669.8 33.2 %all-reduce.11.cloned.1.call-done = f32[448,1024]{1,0:T(8,128)} async-done(((f32[448,1024]{1,0:T(8,128)}), f32[448,1024]{1,0:T(8,128)}) %all-reduce.11.cloned.1.call-update) | async-done | bytes 1835024 | tf_op jit(solution)/shard_map/while/body/eval_jaxpr/psum | solution.py:311
  709.2 14.1 %multiply_reduce_fusion.13 = (f32[2,448]{1,0:T(2,128)S(1)}, f32[2,448,3584]{2,1,0:T(8,128)}) fusion(f32[2,448,3584]{2,1,0:T(8,128)} %copy-done, f32[2,448]{1,0:T(2,128)S(1)} %log_add_fusion.2, bf16[56,2,8,128]{3,2,1,0:T(8,128)(2,1)S(1)} %fusion.336, bf16[3584,256]{1,0:T(8,128)(2,1)} %copy-done.9), kind=kOutput, calls=%fused_computation.10.clone.1 | convolution fusion | flops 831716480 | bytes 27761664 | tf_op jit(solution)/shard_map/while/body/eval_jaxpr/qhd,khd->hqk/dot_general | solution.py:322
  723.7 9.0 multiply_reduce_fusion.14
  748.5 5.8 collective-permute-start.11
  757.5 41.3 %collective-permute-done.11 = bf16[448,256]{0,1:T(8,128)(2,1)S(1)} collective-permute-done((bf16[448,256]{0,1:T(8,128)(2,1)S(1)}, bf16[448,256]{0,1:T(8,128)(2,1)S(1)}, u32[]{:S(2)}, u32[]{:S(2)}) %collective-permute-start.11) | collective-permute-done | bytes 229408 | tf_op jit(solution)/shard_map/while/body/eval_jaxpr/ppermute | solution.py:22
  800.1 5.0 collective-permute-start.13
  806.0 15.1 %collective-permute-done.13 = bf16[448,256]{0,1:T(8,128)(2,1)S(1)} collective-permute-done((bf16[448,256]{0,1:T(8,128)(2,1)S(1)}, bf16[448,256]{0,1:T(8,128)(2,1)S(1)}, u32[]{:S(2)}, u32[]{:S(2)}) %collective-permute-start.13) | collective-permute-done | bytes 229408 | tf_op jit(solution)/shard_map/while/body/eval_jaxpr/ppermute | solution.py:22
  821.0 5.1 collective-permute-start.6
  828.2 5.4 collective-permute-start.8
  835.9 4.5 fusion.350
  863.5 4.4 dynamic_update_slice.57
  867.9 5.0 select_add_fusion.8
  873.0 5.9 select_add_fusion.6
  878.9 5.7 select_add_fusion.7
  897.4 100.2 %all-reduce.13.cloned.1.call-done = (f32[1344,1024]{1,0:T(8,128)}, f32[448,1024]{1,0:T(8,128)}) async-done(((f32[1344,1024]{1,0:T(8,128)}, f32[448,1024]{1,0:T(8,128)}), (f32[1344,1024]{1,0:T(8,128)}, f32[448,1024]{1,0:T(8,128)})) %all-reduce.13.cloned.1.call-update) | async-done | bytes 7340048 | tf_op jit(solution)/shard_map/while/body/eval_jaxpr/psum | solution.py:396
  997.7 5.1 fusion.352
  1037.6 11.3 copy.98
  1048.9 115.0 %shard_map.280 = f32[128,4096]{1,0:T(8,128)S(1)} custom-call(bf16[2,2,2,128,4096]{4,3,2,1,0:T(8,128)(2,1)} %bitcast.421), custom_call_target="tpu_custom_call" | custom-call | tf_op jit(solution)/shard_map/pallas_call | solution.py:139
  1165.2 20.3 %psum.57 = f32[2]{0:T(128)} all-reduce(f32[2]{0:T(128)S(1)} %copy-done.76), channel_id=1, replica_groups=mesh['seq'=8,'tp'=4] {'seq'}, use_global_device_ids=true, to_apply=%region_26.27 | all-reduce | flops 2 | bytes 16 | tf_op jit(solution)/shard_map/psum | solution.py:459
  (707 shorter events, 344.1 us)
Async XLA Ops:
  10.8 134.8 %all-reduce.9.cloned.1.call-start = ((), (), s32[]{:S(2)}) async-start(), calls=%async_computation | async-start | bytes 3670016 | tf_op jit(solution)/shard_map/while/body/eval_jaxpr/psum | solution.py:284
  20.0 41.4 %collective-permute-start = (bf16[1344,256]{1,0:T(8,128)(2,1)S(1)}, bf16[1344,256]{1,0:T(8,128)(2,1)S(1)}, u32[]{:S(2)}, u32[]{:S(2)}) collective-permute-start(bf16[1344,256]{1,0:T(8,128)(2,1)S(1)} %convolution_convert_fusion.8), channel_id=1, source_target_pairs={{0,4},{4,8},{8,12},{12,16},{16,20},{20,24},{24,28},{1,5},{5,9},{9,... | collective-permute-start | bytes 2064392 | tf_op jit(solution)/shard_map/while/body/eval_jaxpr/ppermute | solution.py:22
  24.9 36.6 %collective-permute-start.1 = (bf16[896,256]{1,0:T(8,128)(2,1)S(1)}, bf16[896,256]{1,0:T(8,128)(2,1)S(1)}, u32[]{:S(2)}, u32[]{:S(2)}) collective-permute-start(bf16[896,256]{1,0:T(8,128)(2,1)S(1)} %slice.793), channel_id=1, source_target_pairs={{4,0},{8,4},{12,8},{16,12},{20,16},{24,20},{28,24},{5,1},{9,5},{13... | collective-permute-start | bytes 1376264 | tf_op jit(solution)/shard_map/while/body/eval_jaxpr/ppermute | solution.py:22
  27.2 47.8 %collective-permute-start.2 = (bf16[1344,256]{1,0:T(8,128)(2,1)S(1)}, bf16[1344,256]{1,0:T(8,128)(2,1)S(1)}, u32[]{:S(2)}, u32[]{:S(2)}) collective-permute-start(bf16[1344,256]{1,0:T(8,128)(2,1)S(1)} %convolution_convert_fusion.9), channel_id=1, source_target_pairs={{0,4},{4,8},{8,12},{12,16},{16,20},{20,24},{24,28},{1,5},{5,9},{9,... | collective-permute-start | bytes 2064392 | tf_op jit(solution)/shard_map/while/body/eval_jaxpr/ppermute | solution.py:22
  32.7 56.1 %collective-permute-start.3 = (bf16[896,256]{1,0:T(8,128)(2,1)}, bf16[896,256]{1,0:T(8,128)(2,1)}, u32[]{:S(2)}, u32[]{:S(2)}) collective-permute-start(bf16[896,256]{1,0:T(8,128)(2,1)} %slice.794), channel_id=1, source_target_pairs={{4,0},{8,4},{12,8},{16,12},{20,16},{24,20},{28,24},{5,1},{9,5},{13... | collective-permute-start | bytes 1376264 | tf_op jit(solution)/shard_map/while/body/eval_jaxpr/ppermute | solution.py:22
  34.6 80.6 %collective-permute-start.14 = (bf16[19,1024]{1,0:T(8,128)(2,1)}, bf16[19,1024]{1,0:T(8,128)(2,1)}, u32[]{:S(2)}, u32[]{:S(2)}) collective-permute-start(bf16[19,1024]{1,0:T(8,128)(2,1)} %dynamic-slice_bitcast_fusion.9), channel_id=1, source_target_pairs={{4,0},{8,4},{12,8},{16,12},{20,16},{24,20},{28,24},{5,1},{9,5},{13... | collective-permute-start | bytes 116744 | tf_op jit(solution)/shard_map/while/body/eval_jaxpr/ppermute | solution.py:22
  97.1 106.0 %all-reduce.11.cloned.1.call-start = ((), (), s32[]{:S(2)}) async-start(), calls=%async_computation.1 | async-start | bytes 3670016 | tf_op jit(solution)/shard_map/while/body/eval_jaxpr/psum | solution.py:311
  105.8 57.2 %collective-permute-start.15 = (bf16[19,1024]{1,0:T(8,128)(2,1)}, bf16[19,1024]{1,0:T(8,128)(2,1)}, u32[]{:S(2)}, u32[]{:S(2)}) collective-permute-start(bf16[19,1024]{1,0:T(8,128)(2,1)} %slice.797), channel_id=1, source_target_pairs={{0,4},{4,8},{8,12},{12,16},{16,20},{20,24},{24,28},{1,5},{5,9},{9,... | collective-permute-start | bytes 116744 | tf_op jit(solution)/shard_map/while/body/eval_jaxpr/ppermute | solution.py:22
  147.8 58.4 %copy-start.45 = (f32[448]{0:T(512)}, f32[448]{0:T(512)S(1)}, u32[]{:S(2)}) copy-start(f32[448]{0:T(512)S(1)} %broadcast_multiply_fusion.14) | copy-start | bytes 5380 | tf_op jit(solution)/shard_map/while
  148.1 55.0 %copy-start.51 = (f32[448]{0:T(512)}, f32[448]{0:T(512)S(1)}, u32[]{:S(2)}) copy-start(f32[448]{0:T(512)S(1)} %add_rsqrt_fusion.5) | copy-start | bytes 5380 | tf_op jit(solution)/shard_map/while
  155.8 223.2 %all-reduce.15.cloned.1.call-start = ((), (), s32[]{:S(2)}) async-start(), calls=%async_computation.3 | async-start | bytes 1835008 | tf_op jit(solution)/shard_map/while/body/eval_jaxpr/psum | solution.py:293
  169.5 328.3 %all-reduce.13.cloned.1.call-start = ((), (), s32[]{:S(2)}) async-start(), calls=%async_computation.2 | async-start | bytes 14680064 | tf_op jit(solution)/shard_map/while/body/eval_jaxpr/psum | solution.py:396
  244.1 101.6 %collective-permute-start.4 = (f32[448,256]{0,1:T(8,128)}, f32[448,256]{0,1:T(8,128)}, u32[]{:S(2)}, u32[]{:S(2)}) collective-permute-start(f32[448,256]{0,1:T(8,128)} %bitcast.395), channel_id=1, source_target_pairs={{4,0},{8,4},{12,8},{16,12},{20,16},{24,20},{28,24},{5,1},{9,5},{13... | collective-permute-start | bytes 1376264 | tf_op jit(solution)/shard_map/while/body/eval_jaxpr/ppermute | solution.py:22
  245.3 98.4 %collective-permute-start.5 = (f32[448,256]{0,1:T(8,128)}, f32[448,256]{0,1:T(8,128)}, u32[]{:S(2)}, u32[]{:S(2)}) collective-permute-start(f32[448,256]{0,1:T(8,128)} %bitcast.396), channel_id=1, source_target_pairs={{4,0},{8,4},{12,8},{16,12},{20,16},{24,20},{28,24},{5,1},{9,5},{13... | collective-permute-start | bytes 1376264 | tf_op jit(solution)/shard_map/while/body/eval_jaxpr/ppermute | solution.py:22
  247.2 53.0 %collective-permute-start.10 = (f32[448,256]{0,1:T(8,128)S(1)}, f32[448,256]{0,1:T(8,128)S(1)}, u32[]{:S(2)}, u32[]{:S(2)}) collective-permute-start(f32[448,256]{0,1:T(8,128)S(1)} %bitcast.424), channel_id=1, source_target_pairs={{4,0},{8,4},{12,8},{16,12},{20,16},{24,20},{28,24},{5,1},{9,5},{13... | collective-permute-start | bytes 1376264 | tf_op jit(solution)/shard_map/while/body/eval_jaxpr/ppermute | solution.py:22
  248.6 50.3 %collective-permute-start.11 = (bf16[448,256]{0,1:T(8,128)(2,1)S(1)}, bf16[448,256]{0,1:T(8,128)(2,1)S(1)}, u32[]{:S(2)}, u32[]{:S(2)}) collective-permute-start(bf16[448,256]{0,1:T(8,128)(2,1)S(1)} %bitcast.426), channel_id=1, source_target_pairs={{0,4},{4,8},{8,12},{12,16},{16,20},{20,24},{24,28},{1,5},{5,9},{9,... | collective-permute-start | bytes 688136 | tf_op jit(solution)/shard_map/while/body/eval_jaxpr/ppermute | solution.py:22
  254.4 71.8 %collective-permute-start.12 = (f32[448,256]{0,1:T(8,128)S(1)}, f32[448,256]{0,1:T(8,128)S(1)}, u32[]{:S(2)}, u32[]{:S(2)}) collective-permute-start(f32[448,256]{0,1:T(8,128)S(1)} %bitcast.423), channel_id=1, source_target_pairs={{4,0},{8,4},{12,8},{16,12},{20,16},{24,20},{28,24},{5,1},{9,5},{13... | collective-permute-start | bytes 1376264 | tf_op jit(solution)/shard_map/while/body/eval_jaxpr/ppermute | solution.py:22
  298.9 29.4 %collective-permute-start.9 = (f32[448,256]{0,1:T(8,128)S(1)}, f32[448,256]{0,1:T(8,128)S(1)}, u32[]{:S(2)}, u32[]{:S(2)}) collective-permute-start(f32[448,256]{0,1:T(8,128)S(1)} %bitcast.422), channel_id=1, source_target_pairs={{4,0},{8,4},{12,8},{16,12},{20,16},{24,20},{28,24},{5,1},{9,5},{13... | collective-permute-start | bytes 1376264 | tf_op jit(solution)/shard_map/while/body/eval_jaxpr/ppermute | solution.py:22
  300.2 20.9 %collective-permute-start.13 = (bf16[448,256]{0,1:T(8,128)(2,1)S(1)}, bf16[448,256]{0,1:T(8,128)(2,1)S(1)}, u32[]{:S(2)}, u32[]{:S(2)}) collective-permute-start(bf16[448,256]{0,1:T(8,128)(2,1)S(1)} %bitcast.425), channel_id=1, source_target_pairs={{0,4},{4,8},{8,12},{12,16},{16,20},{20,24},{24,28},{1,5},{5,9},{9,... | collective-permute-start | bytes 688136 | tf_op jit(solution)/shard_map/while/body/eval_jaxpr/ppermute | solution.py:22
  321.1 22.6 %collective-permute-start.6 = (bf16[448,256]{0,1:T(8,128)(2,1)}, bf16[448,256]{0,1:T(8,128)(2,1)}, u32[]{:S(2)}, u32[]{:S(2)}) collective-permute-start(bf16[448,256]{0,1:T(8,128)(2,1)} %bitcast.397), channel_id=1, source_target_pairs={{0,4},{4,8},{8,12},{12,16},{16,20},{20,24},{24,28},{1,5},{5,9},{9,... | collective-permute-start | bytes 688136 | tf_op jit(solution)/shard_map/while/body/eval_jaxpr/ppermute | solution.py:22
  326.2 22.2 %collective-permute-start.7 = (f32[448,256]{0,1:T(8,128)}, f32[448,256]{0,1:T(8,128)}, u32[]{:S(2)}, u32[]{:S(2)}) collective-permute-start(f32[448,256]{0,1:T(8,128)} %bitcast.398), channel_id=1, source_target_pairs={{4,0},{8,4},{12,8},{16,12},{20,16},{24,20},{28,24},{5,1},{9,5},{13... | collective-permute-start | bytes 1376264 | tf_op jit(solution)/shard_map/while/body/eval_jaxpr/ppermute | solution.py:22
  328.3 20.1 %collective-permute-start.8 = (bf16[448,256]{0,1:T(8,128)(2,1)}, bf16[448,256]{0,1:T(8,128)(2,1)}, u32[]{:S(2)}, u32[]{:S(2)}) collective-permute-start(bf16[448,256]{0,1:T(8,128)(2,1)} %bitcast.399), channel_id=1, source_target_pairs={{0,4},{4,8},{8,12},{12,16},{16,20},{20,24},{24,28},{1,5},{5,9},{9,... | collective-permute-start | bytes 688136 | tf_op jit(solution)/shard_map/while/body/eval_jaxpr/ppermute | solution.py:22
  387.1 110.6 %copy-start.2 = (bf16[448,1024]{1,0:T(8,128)(2,1)S(1)}, bf16[448,1024]{1,0:T(8,128)(2,1)}, u32[]{:S(2)}) copy-start(bf16[448,1024]{1,0:T(8,128)(2,1)} %copy-done.1) | copy-start | bytes 2752516 | tf_op jit(solution)/shard_map/while
  387.1 110.6 %copy-start.4 = (bf16[448,1024]{1,0:T(8,128)(2,1)S(1)}, bf16[448,1024]{1,0:T(8,128)(2,1)}, u32[]{:S(2)}) copy-start(bf16[448,1024]{1,0:T(8,128)(2,1)} %copy-done.3) | copy-start | bytes 2752516 | tf_op jit(solution)/shard_map/while
  512.9 132.6 %all-reduce.9.cloned.1.call-start = ((), (), s32[]{:S(2)}) async-start(), calls=%async_computation | async-start | bytes 3670016 | tf_op jit(solution)/shard_map/while/body/eval_jaxpr/psum | solution.py:284
  522.1 40.0 %collective-permute-start = (bf16[1344,256]{1,0:T(8,128)(2,1)S(1)}, bf16[1344,256]{1,0:T(8,128)(2,1)S(1)}, u32[]{:S(2)}, u32[]{:S(2)}) collective-permute-start(bf16[1344,256]{1,0:T(8,128)(2,1)S(1)} %convolution_convert_fusion.8), channel_id=1, source_target_pairs={{0,4},{4,8},{8,12},{12,16},{16,20},{20,24},{24,28},{1,5},{5,9},{9,... | collective-permute-start | bytes 2064392 | tf_op jit(solution)/shard_map/while/body/eval_jaxpr/ppermute | solution.py:22
  525.6 36.6 %collective-permute-start.1 = (bf16[896,256]{1,0:T(8,128)(2,1)S(1)}, bf16[896,256]{1,0:T(8,128)(2,1)S(1)}, u32[]{:S(2)}, u32[]{:S(2)}) collective-permute-start(bf16[896,256]{1,0:T(8,128)(2,1)S(1)} %slice.793), channel_id=1, source_target_pairs={{4,0},{8,4},{12,8},{16,12},{20,16},{24,20},{28,24},{5,1},{9,5},{13... | collective-permute-start | bytes 1376264 | tf_op jit(solution)/shard_map/while/body/eval_jaxpr/ppermute | solution.py:22
  527.8 47.5 %collective-permute-start.2 = (bf16[1344,256]{1,0:T(8,128)(2,1)S(1)}, bf16[1344,256]{1,0:T(8,128)(2,1)S(1)}, u32[]{:S(2)}, u32[]{:S(2)}) collective-permute-start(bf16[1344,256]{1,0:T(8,128)(2,1)S(1)} %convolution_convert_fusion.9), channel_id=1, source_target_pairs={{0,4},{4,8},{8,12},{12,16},{16,20},{20,24},{24,28},{1,5},{5,9},{9,... | collective-permute-start | bytes 2064392 | tf_op jit(solution)/shard_map/while/body/eval_jaxpr/ppermute | solution.py:22
  533.4 55.8 %collective-permute-start.3 = (bf16[896,256]{1,0:T(8,128)(2,1)}, bf16[896,256]{1,0:T(8,128)(2,1)}, u32[]{:S(2)}, u32[]{:S(2)}) collective-permute-start(bf16[896,256]{1,0:T(8,128)(2,1)} %slice.794), channel_id=1, source_target_pairs={{4,0},{8,4},{12,8},{16,12},{20,16},{24,20},{28,24},{5,1},{9,5},{13... | collective-permute-start | bytes 1376264 | tf_op jit(solution)/shard_map/while/body/eval_jaxpr/ppermute | solution.py:22
  535.3 80.3 %collective-permute-start.14 = (bf16[19,1024]{1,0:T(8,128)(2,1)}, bf16[19,1024]{1,0:T(8,128)(2,1)}, u32[]{:S(2)}, u32[]{:S(2)}) collective-permute-start(bf16[19,1024]{1,0:T(8,128)(2,1)} %dynamic-slice_bitcast_fusion.9), channel_id=1, source_target_pairs={{4,0},{8,4},{12,8},{16,12},{20,16},{24,20},{28,24},{5,1},{9,5},{13... | collective-permute-start | bytes 116744 | tf_op jit(solution)/shard_map/while/body/eval_jaxpr/ppermute | solution.py:22
  597.5 105.5 %all-reduce.11.cloned.1.call-start = ((), (), s32[]{:S(2)}) async-start(), calls=%async_computation.1 | async-start | bytes 3670016 | tf_op jit(solution)/shard_map/while/body/eval_jaxpr/psum | solution.py:311
  606.1 56.8 %collective-permute-start.15 = (bf16[19,1024]{1,0:T(8,128)(2,1)}, bf16[19,1024]{1,0:T(8,128)(2,1)}, u32[]{:S(2)}, u32[]{:S(2)}) collective-permute-start(bf16[19,1024]{1,0:T(8,128)(2,1)} %slice.797), channel_id=1, source_target_pairs={{0,4},{4,8},{8,12},{12,16},{16,20},{20,24},{24,28},{1,5},{5,9},{9,... | collective-permute-start | bytes 116744 | tf_op jit(solution)/shard_map/while/body/eval_jaxpr/ppermute | solution.py:22
  647.7 58.4 %copy-start.45 = (f32[448]{0:T(512)}, f32[448]{0:T(512)S(1)}, u32[]{:S(2)}) copy-start(f32[448]{0:T(512)S(1)} %broadcast_multiply_fusion.14) | copy-start | bytes 5380 | tf_op jit(solution)/shard_map/while
  655.7 229.0 %all-reduce.15.cloned.1.call-start = ((), (), s32[]{:S(2)}) async-start(), calls=%async_computation.3 | async-start | bytes 1835008 | tf_op jit(solution)/shard_map/while/body/eval_jaxpr/psum | solution.py:293
  669.4 328.3 %all-reduce.13.cloned.1.call-start = ((), (), s32[]{:S(2)}) async-start(), calls=%async_computation.2 | async-start | bytes 14680064 | tf_op jit(solution)/shard_map/while/body/eval_jaxpr/psum | solution.py:396
  744.0 101.6 %collective-permute-start.4 = (f32[448,256]{0,1:T(8,128)}, f32[448,256]{0,1:T(8,128)}, u32[]{:S(2)}, u32[]{:S(2)}) collective-permute-start(f32[448,256]{0,1:T(8,128)} %bitcast.395), channel_id=1, source_target_pairs={{4,0},{8,4},{12,8},{16,12},{20,16},{24,20},{28,24},{5,1},{9,5},{13... | collective-permute-start | bytes 1376264 | tf_op jit(solution)/shard_map/while/body/eval_jaxpr/ppermute | solution.py:22
  745.2 98.4 %collective-permute-start.5 = (f32[448,256]{0,1:T(8,128)}, f32[448,256]{0,1:T(8,128)}, u32[]{:S(2)}, u32[]{:S(2)}) collective-permute-start(f32[448,256]{0,1:T(8,128)} %bitcast.396), channel_id=1, source_target_pairs={{4,0},{8,4},{12,8},{16,12},{20,16},{24,20},{28,24},{5,1},{9,5},{13... | collective-permute-start | bytes 1376264 | tf_op jit(solution)/shard_map/while/body/eval_jaxpr/ppermute | solution.py:22
  747.1 53.0 %collective-permute-start.10 = (f32[448,256]{0,1:T(8,128)S(1)}, f32[448,256]{0,1:T(8,128)S(1)}, u32[]{:S(2)}, u32[]{:S(2)}) collective-permute-start(f32[448,256]{0,1:T(8,128)S(1)} %bitcast.424), channel_id=1, source_target_pairs={{4,0},{8,4},{12,8},{16,12},{20,16},{24,20},{28,24},{5,1},{9,5},{13... | collective-permute-start | bytes 1376264 | tf_op jit(solution)/shard_map/while/body/eval_jaxpr/ppermute | solution.py:22
  748.5 50.3 %collective-permute-start.11 = (bf16[448,256]{0,1:T(8,128)(2,1)S(1)}, bf16[448,256]{0,1:T(8,128)(2,1)S(1)}, u32[]{:S(2)}, u32[]{:S(2)}) collective-permute-start(bf16[448,256]{0,1:T(8,128)(2,1)S(1)} %bitcast.426), channel_id=1, source_target_pairs={{0,4},{4,8},{8,12},{12,16},{16,20},{20,24},{24,28},{1,5},{5,9},{9,... | collective-permute-start | bytes 688136 | tf_op jit(solution)/shard_map/while/body/eval_jaxpr/ppermute | solution.py:22
  754.3 71.8 %collective-permute-start.12 = (f32[448,256]{0,1:T(8,128)S(1)}, f32[448,256]{0,1:T(8,128)S(1)}, u32[]{:S(2)}, u32[]{:S(2)}) collective-permute-start(f32[448,256]{0,1:T(8,128)S(1)} %bitcast.423), channel_id=1, source_target_pairs={{4,0},{8,4},{12,8},{16,12},{20,16},{24,20},{28,24},{5,1},{9,5},{13... | collective-permute-start | bytes 1376264 | tf_op jit(solution)/shard_map/while/body/eval_jaxpr/ppermute | solution.py:22
  798.8 29.4 %collective-permute-start.9 = (f32[448,256]{0,1:T(8,128)S(1)}, f32[448,256]{0,1:T(8,128)S(1)}, u32[]{:S(2)}, u32[]{:S(2)}) collective-permute-start(f32[448,256]{0,1:T(8,128)S(1)} %bitcast.422), channel_id=1, source_target_pairs={{4,0},{8,4},{12,8},{16,12},{20,16},{24,20},{28,24},{5,1},{9,5},{13... | collective-permute-start | bytes 1376264 | tf_op jit(solution)/shard_map/while/body/eval_jaxpr/ppermute | solution.py:22
  800.1 20.9 %collective-permute-start.13 = (bf16[448,256]{0,1:T(8,128)(2,1)S(1)}, bf16[448,256]{0,1:T(8,128)(2,1)S(1)}, u32[]{:S(2)}, u32[]{:S(2)}) collective-permute-start(bf16[448,256]{0,1:T(8,128)(2,1)S(1)} %bitcast.425), channel_id=1, source_target_pairs={{0,4},{4,8},{8,12},{12,16},{16,20},{20,24},{24,28},{1,5},{5,9},{9,... | collective-permute-start | bytes 688136 | tf_op jit(solution)/shard_map/while/body/eval_jaxpr/ppermute | solution.py:22
  821.0 22.6 %collective-permute-start.6 = (bf16[448,256]{0,1:T(8,128)(2,1)}, bf16[448,256]{0,1:T(8,128)(2,1)}, u32[]{:S(2)}, u32[]{:S(2)}) collective-permute-start(bf16[448,256]{0,1:T(8,128)(2,1)} %bitcast.397), channel_id=1, source_target_pairs={{0,4},{4,8},{8,12},{12,16},{16,20},{20,24},{24,28},{1,5},{5,9},{9,... | collective-permute-start | bytes 688136 | tf_op jit(solution)/shard_map/while/body/eval_jaxpr/ppermute | solution.py:22
  826.1 22.2 %collective-permute-start.7 = (f32[448,256]{0,1:T(8,128)}, f32[448,256]{0,1:T(8,128)}, u32[]{:S(2)}, u32[]{:S(2)}) collective-permute-start(f32[448,256]{0,1:T(8,128)} %bitcast.398), channel_id=1, source_target_pairs={{4,0},{8,4},{12,8},{16,12},{20,16},{24,20},{28,24},{5,1},{9,5},{13... | collective-permute-start | bytes 1376264 | tf_op jit(solution)/shard_map/while/body/eval_jaxpr/ppermute | solution.py:22
  828.2 20.1 %collective-permute-start.8 = (bf16[448,256]{0,1:T(8,128)(2,1)}, bf16[448,256]{0,1:T(8,128)(2,1)}, u32[]{:S(2)}, u32[]{:S(2)}) collective-permute-start(bf16[448,256]{0,1:T(8,128)(2,1)} %bitcast.399), channel_id=1, source_target_pairs={{0,4},{4,8},{8,12},{12,16},{16,20},{20,24},{24,28},{1,5},{5,9},{9,... | collective-permute-start | bytes 688136 | tf_op jit(solution)/shard_map/while/body/eval_jaxpr/ppermute | solution.py:22
  894.0 103.6 %copy-start.2 = (bf16[448,1024]{1,0:T(8,128)(2,1)S(1)}, bf16[448,1024]{1,0:T(8,128)(2,1)}, u32[]{:S(2)}) copy-start(bf16[448,1024]{1,0:T(8,128)(2,1)} %copy-done.1) | copy-start | bytes 2752516 | tf_op jit(solution)/shard_map/while
  894.0 103.6 %copy-start.4 = (bf16[448,1024]{1,0:T(8,128)(2,1)S(1)}, bf16[448,1024]{1,0:T(8,128)(2,1)}, u32[]{:S(2)}) copy-start(bf16[448,1024]{1,0:T(8,128)(2,1)} %copy-done.3) | copy-start | bytes 2752516 | tf_op jit(solution)/shard_map/while
  1048.9 116.4 %copy-start.76 = (f32[2]{0:T(128)S(1)}, f32[2]{0:T(128)}, u32[]{:S(2)}) copy-start(f32[2]{0:T(128)} %get-tuple-element.528) | copy-start | bytes 28
  (180 other events, 1059.2 us)
Sparse Core Ops, SparseCore 0:
  97.2 48.3 all-reduce.8
  155.9 47.1 all-reduce.10
  205.5 35.3 all-reduce.14
  360.6 137.0 all-reduce.12
  597.6 47.8 all-reduce.8
  655.8 47.1 all-reduce.10
  705.4 35.3 all-reduce.14
  860.5 137.1 all-reduce.12
